TPU v7x, 32 devices: a whole 2x2x4 slice. The times are simulated.
32 devices in a mesh: rows: 16 (over z, y, x), layer: 2 (over core).
Axes of the slice: x: 2, y: 2, z: 4, core: 2. Of those that a mesh axis runs over, the one named last changes fastest.
Arguments:
- density: bfloat16 [256, 33, 64, 64], P('rows'), as said below
- col_index: int32 [256, 33], replicated, may hold values from 0 to 255, as said below
- counts: int32 [256], replicated, may hold values from 1 to 33, as said below
- domain: int32 [256], replicated, may hold values from 0 to 63
Outputs:
- square: bfloat16 [256, 33, 64, 64], P(('rows', 'layer'))
- populations: float32 [64, 64], P(('rows', 'layer'))
- traces: float32 [2], replicated
Inputs may be any that keep to these rules, and one draw needn't show every extreme that they name: `col_index`: the pattern is symmetric, holds every diagonal block, and every stored column lies within 16 block rows of its row, counted cyclically over 256. The first counts[i] slots of row i hold distinct columns in rising order of their cyclic distance from -16 to 16; the other slots hold further distinct columns within that reach. `counts`: some row holds all 33 slots. `density`: block X[j, i] is the transpose of X[i, j]; slots that are not live hold zeros.
All inputs are finite; a program needn't handle non-finite values.
Results may differ from a plain program's by a relative error of at most 0.0018.
Values may be sent and summed in bfloat16 or wider, within the bound.
No kernel may reach another device: no remote copies, remote signals or barrier semaphores. Data moves between devices by JAX's collectives and lax.ppermute only.
A program may use at most 192 MiB of HBM per device.

v0:
```python
import jax
import jax.numpy as jnp
from jax import lax
from jax.sharding import PartitionSpec as P

DOM_DEV = 2


def padded(value, sides, width):
    for axis, dim in sides:
        devices, length = (lax.axis_size(axis), value.shape[dim])
        up = [(i, (i + 1) % devices) for i in range(devices)]
        down = [(j, i) for i, j in up]
        last = lax.slice_in_dim(value, length - width, length, axis=dim)
        leading = lax.slice_in_dim(value, 0, width, axis=dim)
        before = lax.ppermute(last, axis, up)
        after = lax.ppermute(leading, axis, down)
        value = jnp.concatenate([before, value, after], axis=dim)
    return value


def per_device(density, col_index, counts, domain):
    per_dev = density.shape[0]
    capacity = density.shape[1]
    width = density.shape[2]
    block_rows = col_index.shape[0]
    radius = (capacity - 1) // 2
    half_rows = per_dev // 2
    start_row = lax.axis_index("rows") * per_dev
    layer_id = lax.axis_index("layer")
    banded = padded(density, (("rows", 0),), radius)
    slot_range = jnp.arange(capacity, dtype=jnp.int32)

    def row_block(local, slot_ids):
        row_id = start_row + local
        row_cols = lax.dynamic_index_in_dim(col_index, row_id, 0, keepdims=False)
        row_count = lax.dynamic_index_in_dim(counts, row_id, 0, keepdims=False)
        slot_safe = jnp.minimum(slot_ids, capacity - 1)
        slot_live = (slot_ids < capacity) & (slot_safe < row_count)
        partner = row_cols[slot_safe]
        offset = (partner - row_id + radius) % block_rows - radius
        position = local + radius + offset
        partner_rows = banded[position]
        partner_cols = col_index[partner]
        partner_count = counts[partner]
        select = partner_cols[:, None, :] == row_cols[None, :, None]
        select = select & (slot_range[None, None, :] < partner_count[:, None, None])
        select = select & slot_live[:, None, None] & (slot_range < row_count)[None, :, None]
        picked = jnp.einsum(
            "amb,abxy->amxy",
            select.astype(jnp.bfloat16),
            partner_rows,
            preferred_element_type=jnp.float32,
        ).astype(jnp.bfloat16)
        left_blocks = lax.dynamic_index_in_dim(density, local, 0, keepdims=False)[slot_safe]
        return jnp.einsum("apx,amxy->mpy", left_blocks, picked, preferred_element_type=jnp.float32)

    slot_ids = jnp.arange(capacity, dtype=jnp.int32)
    square = lax.map(
        lambda local: row_block(layer_id * half_rows + local, slot_ids),
        jnp.arange(half_rows, dtype=jnp.int32),
    ).astype(jnp.bfloat16)
    owned = start_row + layer_id * half_rows + jnp.arange(half_rows, dtype=jnp.int32)
    diag_mask = (col_index[owned] == owned[:, None]) & (
        slot_range[None, :] < counts[owned][:, None]
    )
    diag_mask = diag_mask.astype(jnp.float32)[:, :, None]
    diag_square = jnp.sum(
        diag_mask * jnp.diagonal(square, axis1=2, axis2=3).astype(jnp.float32), axis=1
    )
    owned_blocks = lax.dynamic_slice_in_dim(density, layer_id * half_rows, half_rows, 0)
    diag_density = jnp.sum(
        diag_mask * jnp.diagonal(owned_blocks, axis1=2, axis2=3).astype(jnp.float32), axis=1
    )
    domain_total = lax.axis_size("rows") * lax.axis_size("layer") * DOM_DEV
    onehot = (domain[owned][:, None] == jnp.arange(domain_total, dtype=jnp.int32)[None, :]).astype(
        jnp.float32
    )
    contrib = jnp.dot(
        onehot.T, diag_square, precision=lax.Precision.HIGHEST, preferred_element_type=jnp.float32
    )
    populations = lax.psum_scatter(contrib, ("rows", "layer"), scatter_dimension=0, tiled=True)
    trace_sums = lax.psum((jnp.sum(diag_density), jnp.sum(diag_square)), ("rows", "layer"))
    traces = jnp.stack([trace_sums[0], trace_sums[1]]) / (block_rows * width)
    return (square, populations, traces)


def solution(mesh):
    placed = (P("rows", None, None, None), P(), P(), P())
    return jax.shard_map(
        per_device,
        mesh=mesh,
        in_specs=placed,
        out_specs=(P(("rows", "layer"), None, None, None), P(("rows", "layer"), None), P()),
        check_vma=False,
    )
```

profile of v0, /device:TPU:0, one launch (start us, length us, event | category | flops | bytes accessed | tf_op | source)
XLA Modules:
  0.0 910.7 jit_solution(13786787781242334886)
XLA Ops:
  32.3 161.0 %collective-permute-done.1 = bf16[16,33,64,64]{3,2,1,0:T(8,128)(2,1)} collective-permute-done((bf16[16,33,64,64]{3,2,1,0:T(8,128)(2,1)}, bf16[16,33,64,64]{3,2,1,0:T(8,128)(2,1)}, u32[]{:S(2)}, u32[]{:S(2)}) %collective-permute-start.1) | collective-permute-done | bytes 4325408 | tf_op jit(solution)/shard_map/ppermute | solution.py:17
  193.3 183.2 %collective-permute-done = bf16[16,33,64,64]{3,2,1,0:T(8,128)(2,1)} collective-permute-done((bf16[16,33,64,64]{3,2,1,0:T(8,128)(2,1)}, bf16[16,33,64,64]{3,2,1,0:T(8,128)(2,1)}, u32[]{:S(2)}, u32[]{:S(2)}) %collective-permute-start) | collective-permute-done | bytes 4325408 | tf_op jit(solution)/shard_map/ppermute | solution.py:16
  376.6 18.6 %pad_maximum_fusion = bf16[48,33,64,64]{3,2,1,0:T(8,128)(2,1)} fusion(bf16[16,33,64,64]{3,2,1,0:T(8,128)(2,1)} %collective-permute-done.1, bf16[16,33,64,64]{3,2,1,0:T(8,128)(2,1)} %param.6, bf16[16,33,64,64]{3,2,1,0:T(8,128)(2,1)} %collective-permute-done), kind=kLoop, calls=%fused_computation.54 | loop fusion | flops 12976128 | bytes 25952256 | tf_op jit(solution)/shard_map/concatenate | solution.py:18
  395.2 441.3 %while.15 = (s32[]{:T(128)}, bf16[8,33,64,64]{2,3,1,0:T(8,128)(2,1)}, s32[8]{0:T(128)S(1)}, s32[]{:T(128)}, s32[]{:T(128)}, /*index=5*/s32[256,33]{1,0:T(8,128)S...) while((s32[]{:T(128)}, ...), condition=%wide.region_1.2_spmd.clone.clone, body=%wide.region_0.1_spmd.clone.clone.sunk | while | flops 869954944 | bytes 59774832 | solution.py:59
  397.2 16.1 %gather_fusion.1 = bf16[33,33,64,64]{3,2,1,0:T(8,128)(2,1)} fusion(bf16[48,33,64,64]{3,2,1,0:T(8,128)(2,1)} %get-tuple-element.385, s32[1024]{0:T(1024)S(1)} %get-tuple-element.348), kind=kCustom, calls=%fused_computation.3.clone.clone.1 | custom fusion | bytes 17842308 | tf_op jit(solution)/shard_map/while/body/eval_jaxpr/gather | solution.py:43
  416.0 21.6 %fusion.61 = bf16[33,33,64,64]{3,1,2,0:T(8,128)(2,1)} fusion(bf16[33,33,64,64]{3,2,1,0:T(8,128)(2,1)} %gather_fusion.1, s32[33,33]{1,0:T(8,128)S(1)} %gather_fusion.2, s32[33]{0:T(128)S(1)} %fusion.58, pred[33]{0:T(512)(128)(4,1)S(1)} %get-tuple-element.350, pred[33]{0:T(512)(128)(4,1)S(1)} %get-tuple-element.351, ...), kind=kOutput, calls=%fused_computation.15.clone.1 | convolution fusion | flops 299000192 | bytes 17847820 | tf_op jit(solution)/shard_map/while/body/eval_jaxpr/amb,abxy->amxy/dot_general | solution.py:49
  439.3 11.1 %fusion.62 = bf16[8,33,64,64]{2,3,1,0:T(8,128)(2,1)} fusion(bf16[8,33,64,64]{2,3,1,0:T(8,128)(2,1)} %get-tuple-element.366, s32[]{:T(128)S(6)} %copy.42, bf16[33,33,64,64]{3,1,2,0:T(8,128)(2,1)} %fusion.61, bf16[33,64,64]{2,1,0:T(8,128)(2,1)S(1)} %gather_fusion.4), kind=kOutput, calls=%fused_computation.17.clone.1 | convolution fusion | flops 570949632 | bytes 22978564 | tf_op jit(solution)/shard_map/while/body/eval_jaxpr/apx,amxy->mpy/dot_general | solution.py:56
  452.4 16.1 %gather_fusion.1 = bf16[33,33,64,64]{3,2,1,0:T(8,128)(2,1)} fusion(bf16[48,33,64,64]{3,2,1,0:T(8,128)(2,1)} %get-tuple-element.385, s32[1024]{0:T(1024)S(1)} %get-tuple-element.348), kind=kCustom, calls=%fused_computation.3.clone.clone.1 | custom fusion | bytes 17842308 | tf_op jit(solution)/shard_map/while/body/eval_jaxpr/gather | solution.py:43
  471.1 21.6 %fusion.61 = bf16[33,33,64,64]{3,1,2,0:T(8,128)(2,1)} fusion(bf16[33,33,64,64]{3,2,1,0:T(8,128)(2,1)} %gather_fusion.1, s32[33,33]{1,0:T(8,128)S(1)} %gather_fusion.2, s32[33]{0:T(128)S(1)} %fusion.58, pred[33]{0:T(512)(128)(4,1)S(1)} %get-tuple-element.350, pred[33]{0:T(512)(128)(4,1)S(1)} %get-tuple-element.351, ...), kind=kOutput, calls=%fused_computation.15.clone.1 | convolution fusion | flops 299000192 | bytes 17847820 | tf_op jit(solution)/shard_map/while/body/eval_jaxpr/amb,abxy->amxy/dot_general | solution.py:49
  494.5 11.1 %fusion.62 = bf16[8,33,64,64]{2,3,1,0:T(8,128)(2,1)} fusion(bf16[8,33,64,64]{2,3,1,0:T(8,128)(2,1)} %get-tuple-element.366, s32[]{:T(128)S(6)} %copy.42, bf16[33,33,64,64]{3,1,2,0:T(8,128)(2,1)} %fusion.61, bf16[33,64,64]{2,1,0:T(8,128)(2,1)S(1)} %gather_fusion.4), kind=kOutput, calls=%fused_computation.17.clone.1 | convolution fusion | flops 570949632 | bytes 22978564 | tf_op jit(solution)/shard_map/while/body/eval_jaxpr/apx,amxy->mpy/dot_general | solution.py:56
  507.6 16.1 %gather_fusion.1 = bf16[33,33,64,64]{3,2,1,0:T(8,128)(2,1)} fusion(bf16[48,33,64,64]{3,2,1,0:T(8,128)(2,1)} %get-tuple-element.385, s32[1024]{0:T(1024)S(1)} %get-tuple-element.348), kind=kCustom, calls=%fused_computation.3.clone.clone.1 | custom fusion | bytes 17842308 | tf_op jit(solution)/shard_map/while/body/eval_jaxpr/gather | solution.py:43
  526.3 21.6 %fusion.61 = bf16[33,33,64,64]{3,1,2,0:T(8,128)(2,1)} fusion(bf16[33,33,64,64]{3,2,1,0:T(8,128)(2,1)} %gather_fusion.1, s32[33,33]{1,0:T(8,128)S(1)} %gather_fusion.2, s32[33]{0:T(128)S(1)} %fusion.58, pred[33]{0:T(512)(128)(4,1)S(1)} %get-tuple-element.350, pred[33]{0:T(512)(128)(4,1)S(1)} %get-tuple-element.351, ...), kind=kOutput, calls=%fused_computation.15.clone.1 | convolution fusion | flops 299000192 | bytes 17847820 | tf_op jit(solution)/shard_map/while/body/eval_jaxpr/amb,abxy->amxy/dot_general | solution.py:49
  562.7 16.1 %gather_fusion.1 = bf16[33,33,64,64]{3,2,1,0:T(8,128)(2,1)} fusion(bf16[48,33,64,64]{3,2,1,0:T(8,128)(2,1)} %get-tuple-element.385, s32[1024]{0:T(1024)S(1)} %get-tuple-element.348), kind=kCustom, calls=%fused_computation.3.clone.clone.1 | custom fusion | bytes 17842308 | tf_op jit(solution)/shard_map/while/body/eval_jaxpr/gather | solution.py:43
  581.5 21.6 %fusion.61 = bf16[33,33,64,64]{3,1,2,0:T(8,128)(2,1)} fusion(bf16[33,33,64,64]{3,2,1,0:T(8,128)(2,1)} %gather_fusion.1, s32[33,33]{1,0:T(8,128)S(1)} %gather_fusion.2, s32[33]{0:T(128)S(1)} %fusion.58, pred[33]{0:T(512)(128)(4,1)S(1)} %get-tuple-element.350, pred[33]{0:T(512)(128)(4,1)S(1)} %get-tuple-element.351, ...), kind=kOutput, calls=%fused_computation.15.clone.1 | convolution fusion | flops 299000192 | bytes 17847820 | tf_op jit(solution)/shard_map/while/body/eval_jaxpr/amb,abxy->amxy/dot_general | solution.py:49
  617.9 16.1 %gather_fusion.1 = bf16[33,33,64,64]{3,2,1,0:T(8,128)(2,1)} fusion(bf16[48,33,64,64]{3,2,1,0:T(8,128)(2,1)} %get-tuple-element.385, s32[1024]{0:T(1024)S(1)} %get-tuple-element.348), kind=kCustom, calls=%fused_computation.3.clone.clone.1 | custom fusion | bytes 17842308 | tf_op jit(solution)/shard_map/while/body/eval_jaxpr/gather | solution.py:43
  636.6 21.6 %fusion.61 = bf16[33,33,64,64]{3,1,2,0:T(8,128)(2,1)} fusion(bf16[33,33,64,64]{3,2,1,0:T(8,128)(2,1)} %gather_fusion.1, s32[33,33]{1,0:T(8,128)S(1)} %gather_fusion.2, s32[33]{0:T(128)S(1)} %fusion.58, pred[33]{0:T(512)(128)(4,1)S(1)} %get-tuple-element.350, pred[33]{0:T(512)(128)(4,1)S(1)} %get-tuple-element.351, ...), kind=kOutput, calls=%fused_computation.15.clone.1 | convolution fusion | flops 299000192 | bytes 17847820 | tf_op jit(solution)/shard_map/while/body/eval_jaxpr/amb,abxy->amxy/dot_general | solution.py:49
  673.1 16.1 %gather_fusion.1 = bf16[33,33,64,64]{3,2,1,0:T(8,128)(2,1)} fusion(bf16[48,33,64,64]{3,2,1,0:T(8,128)(2,1)} %get-tuple-element.385, s32[1024]{0:T(1024)S(1)} %get-tuple-element.348), kind=kCustom, calls=%fused_computation.3.clone.clone.1 | custom fusion | bytes 17842308 | tf_op jit(solution)/shard_map/while/body/eval_jaxpr/gather | solution.py:43
  691.8 21.6 %fusion.61 = bf16[33,33,64,64]{3,1,2,0:T(8,128)(2,1)} fusion(bf16[33,33,64,64]{3,2,1,0:T(8,128)(2,1)} %gather_fusion.1, s32[33,33]{1,0:T(8,128)S(1)} %gather_fusion.2, s32[33]{0:T(128)S(1)} %fusion.58, pred[33]{0:T(512)(128)(4,1)S(1)} %get-tuple-element.350, pred[33]{0:T(512)(128)(4,1)S(1)} %get-tuple-element.351, ...), kind=kOutput, calls=%fused_computation.15.clone.1 | convolution fusion | flops 299000192 | bytes 17847820 | tf_op jit(solution)/shard_map/while/body/eval_jaxpr/amb,abxy->amxy/dot_general | solution.py:49
  728.2 16.1 %gather_fusion.1 = bf16[33,33,64,64]{3,2,1,0:T(8,128)(2,1)} fusion(bf16[48,33,64,64]{3,2,1,0:T(8,128)(2,1)} %get-tuple-element.385, s32[1024]{0:T(1024)S(1)} %get-tuple-element.348), kind=kCustom, calls=%fused_computation.3.clone.clone.1 | custom fusion | bytes 17842308 | tf_op jit(solution)/shard_map/while/body/eval_jaxpr/gather | solution.py:43
  747.0 21.6 %fusion.61 = bf16[33,33,64,64]{3,1,2,0:T(8,128)(2,1)} fusion(bf16[33,33,64,64]{3,2,1,0:T(8,128)(2,1)} %gather_fusion.1, s32[33,33]{1,0:T(8,128)S(1)} %gather_fusion.2, s32[33]{0:T(128)S(1)} %fusion.58, pred[33]{0:T(512)(128)(4,1)S(1)} %get-tuple-element.350, pred[33]{0:T(512)(128)(4,1)S(1)} %get-tuple-element.351, ...), kind=kOutput, calls=%fused_computation.15.clone.1 | convolution fusion | flops 299000192 | bytes 17847820 | tf_op jit(solution)/shard_map/while/body/eval_jaxpr/amb,abxy->amxy/dot_general | solution.py:49
  783.4 16.1 %gather_fusion.1 = bf16[33,33,64,64]{3,2,1,0:T(8,128)(2,1)} fusion(bf16[48,33,64,64]{3,2,1,0:T(8,128)(2,1)} %get-tuple-element.385, s32[1024]{0:T(1024)S(1)} %get-tuple-element.348), kind=kCustom, calls=%fused_computation.3.clone.clone.1 | custom fusion | bytes 17842308 | tf_op jit(solution)/shard_map/while/body/eval_jaxpr/gather | solution.py:43
  802.1 21.6 %fusion.61 = bf16[33,33,64,64]{3,1,2,0:T(8,128)(2,1)} fusion(bf16[33,33,64,64]{3,2,1,0:T(8,128)(2,1)} %gather_fusion.1, s32[33,33]{1,0:T(8,128)S(1)} %gather_fusion.2, s32[33]{0:T(128)S(1)} %fusion.58, pred[33]{0:T(512)(128)(4,1)S(1)} %get-tuple-element.350, pred[33]{0:T(512)(128)(4,1)S(1)} %get-tuple-element.351, ...), kind=kOutput, calls=%fused_computation.15.clone.1 | convolution fusion | flops 299000192 | bytes 17847820 | tf_op jit(solution)/shard_map/while/body/eval_jaxpr/amb,abxy->amxy/dot_general | solution.py:49
  836.5 15.7 %copy.18 = bf16[8,33,64,64]{1,0,3,2:T(8,128)(2,1)} copy(bf16[8,33,64,64]{2,3,1,0:T(8,128)(2,1)} %get-tuple-element.173) | data formatting | bytes 4325376 | tf_op jit(solution)/shard_map/while | solution.py:59
  868.2 40.2 %all-reduce.1 = (f32[64,64]{1,0:T(8,128)S(1)}, f32[1]{0:T(128)}, f32[1]{0:T(128)}) all-reduce(f32[64,64]{1,0:T(8,128)S(1)} %fusion.40, f32[1]{0:T(128)} %bitcast.3, f32[1]{0:T(128)} %bitcast.2), channel_id=2, replica_groups=mesh['rows'=16,'layer'=2] {'rows','layer'}, use_global_device_ids=true, to_apply=%region_3.4.clone | all-reduce | flops 4098 | bytes 32784
  (156 shorter events, 162.1 us)
Async XLA Ops:
  0.6 25.1 %copy-start = (s32[256]{0:T(256)S(1)}, s32[256]{0:T(256)}, u32[]{:S(2)}) copy-start(s32[256]{0:T(256)} %param.9) | copy-start | bytes 3076
  0.6 192.7 %collective-permute-start.1 = (bf16[16,33,64,64]{3,2,1,0:T(8,128)(2,1)}, bf16[16,33,64,64]{3,2,1,0:T(8,128)(2,1)}, u32[]{:S(2)}, u32[]{:S(2)}) collective-permute-start(bf16[16,33,64,64]{3,2,1,0:T(8,128)(2,1)} %param.6), channel_id=1, source_target_pairs={{2,0},{4,2},{6,4},{8,6},{10,8},{12,10},{14,12},{16,14},{18,16},{20... | collective-permute-start | bytes 12976136 | tf_op jit(solution)/shard_map/ppermute | solution.py:17
  7.7 368.9 %collective-permute-start = (bf16[16,33,64,64]{3,2,1,0:T(8,128)(2,1)}, bf16[16,33,64,64]{3,2,1,0:T(8,128)(2,1)}, u32[]{:S(2)}, u32[]{:S(2)}) collective-permute-start(bf16[16,33,64,64]{3,2,1,0:T(8,128)(2,1)} %param.6), channel_id=1, source_target_pairs={{0,2},{2,4},{4,6},{6,8},{8,10},{10,12},{12,14},{14,16},{16,18},{18... | collective-permute-start | bytes 12976136 | tf_op jit(solution)/shard_map/ppermute | solution.py:16
  26.9 4.8 copy-start.3
  32.3 362.9 %copy-start.2 = (s32[256]{0:T(256)S(1)}, s32[256]{0:T(256)}, u32[]{:S(2)}) copy-start(s32[256]{0:T(256)} %param.8) | copy-start | bytes 3076
  836.5 74.1 %copy-start.1 = (s32[256]{0:T(256)S(1)}, s32[256]{0:T(256)}, u32[]{:S(2)}) copy-start(s32[256]{0:T(256)} %param.9) | copy-start | bytes 3076
  852.2 10.8 %copy-start.4 = (s32[64]{0:T(128)S(1)}, s32[64]{0:T(128)}, u32[]{:S(2)}) copy-start(s32[64]{0:T(128)} %copy-done.3) | copy-start | bytes 772
  852.2 15.0 %copy-start.5 = (bf16[64,8,33]{2,1,0:T(8,128)(2,1)S(1)}, bf16[64,8,33]{2,1,0:T(8,128)(2,1)}, u32[]{:S(2)}) copy-start(bf16[64,8,33]{2,1,0:T(8,128)(2,1)} %gather_fusion.9) | copy-start | bytes 101380
  852.2 15.0 %copy-start.6 = (f32[8,33]{1,0:T(8,128)S(1)}, f32[8,33]{1,0:T(8,128)}, u32[]{:S(2)}) copy-start(f32[8,33]{1,0:T(8,128)} %fusion.39) | copy-start | bytes 3172
  852.2 15.7 %copy-start.7 = (s32[8]{0:T(128)S(1)}, s32[8]{0:T(128)}, u32[]{:S(2)}) copy-start(s32[8]{0:T(128)} %gather_fusion.5) | copy-start | bytes 100
where the time goes:
time: 913 us; the launch traced here: 911 us
  waiting for transfers between devices  344 us (38%)
  matrix products  262 us (29%)
  local copies, waits for them, and re-layouts  225 us (25%)
  blocking collectives  40.2 us (4%)
  other arithmetic  27.2 us (3%)
    ppermute x1, waiting for transfers between devices, padded(): before = lax.ppermute(last, axis, up)  183 us
    dot_general x8, matrix products, row_block(): jnp.einsum('amb,abxy->amxy', select.astype(jnp.bfloat16), partner_rows, p...  173 us
    ppermute x1, waiting for transfers between devices, padded(): after = lax.ppermute(leading, axis, down)  161 us
    gather x8, local copies, waits for them, and re-layouts, row_block(): partner_rows = banded[position]  129 us
    dot_general x8, matrix products, row_block(): jnp.einsum('apx,amxy->mpy', left_blocks, picked, preferred_element_type=j...  88.6 us
    unnamed x1, blocking collectives  40.2 us
    unnamed x20, local copies, waits for them, and re-layouts  22.2 us
    concatenate x1, other arithmetic, padded(): value = jnp.concatenate([before, value, after], axis=dim)  18.6 us
  transfers between devices with their start and end apart: 2, of which 2 were waited for; matrix products, arithmetic and copies ran while one was open for 3% of the time, Pallas kernels for 0%

commit v1 on v0

v1 whole, which is shorter than its diff:
```python
import functools

import jax
import jax.numpy as jnp
from jax import lax
from jax.experimental import pallas as pl
from jax.experimental.pallas import tpu as pltpu
from jax.sharding import PartitionSpec as P

DOM_DEV = 2
AXES = ("rows", "layer")
SYM = [(u, t) for u in range(4) for t in range(u, 4)]
FULL = [(u, t) for u in range(4) for t in range(4)]
NT = (((1,), (1,)), ((), ()))
BF = jnp.bfloat16
F32 = jnp.float32
IN_HBM = pl.BlockSpec(memory_space=pltpu.HBM)


def pack_kernel(groups, meta, density, *rest):
    outs, buf, sems = rest[-2 - len(groups) : -2], rest[-2], rest[-1]
    layer = lax.axis_index("layer")
    starts = (8 * layer, 8 * (1 - layer))
    base = 0
    for g, (tiles, near, far) in enumerate(groups):
        row, col = starts[near], starts[far]
        for n, (u, t) in enumerate(tiles):
            for r in range(2):
                for s in range(2):
                    k = row + 2 * u + r
                    slot = meta[k, (col - row) + 2 * t + s - 2 * u - r + 16]
                    at = base + 4 * n + 2 * r + s
                    pltpu.make_async_copy(density.at[k, slot], buf.at[at], sems.at[g]).start()
        base += 4 * len(tiles)
    base = 0
    for g, (tiles, _, _) in enumerate(groups):
        span = buf.at[pl.ds(base, 4 * len(tiles))]
        pltpu.make_async_copy(span, span, sems.at[g]).wait()
        for n in range(len(tiles)):
            for r in range(2):
                at = base + 4 * n + 2 * r
                outs[g][n, 64 * r : 64 * r + 64, :] = jnp.concatenate(
                    [buf[at], buf[at + 1]], axis=1
                )
        base += 4 * len(tiles)


def pack(groups, meta, density, *after):
    sizes = [len(tiles) for tiles, _, _ in groups]
    return pl.pallas_call(
        functools.partial(pack_kernel, groups),
        grid_spec=pltpu.PrefetchScalarGridSpec(
            num_scalar_prefetch=1,
            grid=(1,),
            in_specs=[IN_HBM] * (1 + len(after)),
            out_specs=[pl.BlockSpec((n, 128, 128), lambda i, m: (0, 0, 0)) for n in sizes],
            scratch_shapes=[
                pltpu.VMEM((4 * sum(sizes), 64, 64), BF),
                pltpu.SemaphoreType.DMA((len(sizes),)),
            ],
        ),
        out_shape=[jax.ShapeDtypeStruct((n, 128, 128), BF) for n in sizes],
        compiler_params=pltpu.CompilerParams(vmem_limit_bytes=58 << 20),
        cost_estimate=pl.CostEstimate(
            flops=0, bytes_accessed=sum(sizes) << 17, transcendentals=0
        ),
        name="pack",
    )(meta, density, *after)


def spread(slots, block, own, first, at, k):
    zero = jnp.zeros((64, 64), BF)
    for r in range(2):
        rows = pl.ds(pl.multiple_of(at + 64 * r, 64), 64)
        total = jnp.zeros((64, 128), F32)
        for pp in range(17):
            halves = []
            for s in range(2):
                d = 2 * pp + s - r
                halves.append(block(r, slots[k + r, d]) if 0 <= d <= 32 else zero)
            pair = jnp.concatenate(halves, axis=1)
            own[first + pp, rows, :] = pair
            wide_pair = pair.astype(F32)
            total += wide_pair * wide_pair
        yield r, total


def diag_kernel(meta, domain, rows_ref, _, out_ref, own, sums):
    step = pl.program_id(0)
    layer = lax.axis_index("layer")
    start = 16 * lax.axis_index("rows")
    k = 8 * layer + 2 * step

    @pl.when(step == 0)
    def _():
        out_ref[...] = jnp.zeros_like(out_ref)
        sums[...] = jnp.zeros_like(sums)

        @pl.loop(0, 24)
        def _(p):
            own[p] = jnp.zeros(own.shape[1:], BF)

    eye = lax.broadcasted_iota(jnp.int32, (64, 64), 0) == lax.broadcasted_iota(
        jnp.int32, (64, 64), 1
    )
    sub = lax.broadcasted_iota(jnp.int32, (8, 64), 0)

    def block(r, slot):
        return rows_ref[r, slot]

    for r, total in spread(meta, block, own, 4 * layer + step, 128 * step, k):
        column = jnp.sum(total, axis=1, keepdims=True)
        squares = jnp.sum(jnp.where(eye, column, 0.0), axis=0, keepdims=True)
        squares = squares.astype(BF).astype(F32)
        middle = block(r, meta[k + r, 16]).astype(F32)
        diagonal = jnp.sum(jnp.where(eye, middle, 0.0), axis=0, keepdims=True)
        target = domain[start + k + r]
        owner = target // DOM_DEV
        place = target - owner * DOM_DEV
        out_ref[owner, :, 0:64] = out_ref[owner, :, 0:64] + jnp.where(sub == place, squares, 0.0)
        sums[:, 0:64] = sums[:, 0:64] + jnp.where(
            sub == DOM_DEV, diagonal, jnp.where(sub == DOM_DEV + 1, squares, 0.0)
        )

    @pl.when(step == pl.num_programs(0) - 1)
    def _():
        out_ref[...] = out_ref[...] + sums[...][None]


def diagonals(meta, domain, density, after, devices):
    capacity = density.shape[1]
    return pl.pallas_call(
        diag_kernel,
        grid_spec=pltpu.PrefetchScalarGridSpec(
            num_scalar_prefetch=2,
            grid=(4,),
            in_specs=[
                pl.BlockSpec(
                    (2, capacity, 64, 64),
                    lambda i, m, d: (4 * lax.axis_index("layer") + i, 0, 0, 0),
                ),
                IN_HBM,
            ],
            out_specs=[
                pl.BlockSpec((devices, 8, 128), lambda i, m, d: (0, 0, 0)),
                pl.BlockSpec((24, 512, 128), lambda i, m, d: (0, 0, 0)),
            ],
            scratch_shapes=[pltpu.VMEM((8, 128), F32)],
        ),
        out_shape=[
            jax.ShapeDtypeStruct((devices, 8, 128), F32),
            jax.ShapeDtypeStruct((24, 512, 128), BF),
        ],
        compiler_params=pltpu.CompilerParams(vmem_limit_bytes=54 << 20),
        cost_estimate=pl.CostEstimate(flops=0, bytes_accessed=8 << 20, transcendentals=0),
        name="diagonals",
    )(meta, domain, density, after)


def octant(layer, q):
    return jnp.where(layer == 0, q, 5 - q)


def wide(ref, pair, rows):
    return jnp.concatenate([ref[pair, rows, :], ref[pair + 1, rows, :]], axis=1)


def local_kernel(meta, density, mine, _, part_ref, near_ref, rows_ref, sems, other):
    layer = lax.axis_index("layer")
    sib = 8 * (1 - layer)
    for k in range(8):
        pltpu.make_async_copy(density.at[sib + k], rows_ref.at[k], sems.at[k]).start()

    @pl.loop(0, 24)
    def _(p):
        other[p] = jnp.zeros(other.shape[1:], BF)

    @pl.loop(0, 4)
    def _(u):
        for r in range(2):
            k = 2 * u + r
            pltpu.make_async_copy(density.at[sib + k], rows_ref.at[k], sems.at[k]).wait()

        def block(r, slot):
            return rows_ref[2 * u + r, slot]

        for _ in spread(meta, block, other, 4 * (1 - layer) + u, 128 * u, sib + 2 * u):
            pass

    at = [4 * octant(layer, q) for q in range(5)]
    every = pl.ds(0, 512)

    def put(ref, base, half, value):
        ref[base + 2 * half] = value[:, 0:128].astype(ref.dtype)
        ref[base + 2 * half + 1] = value[:, 128:256].astype(ref.dtype)

    def left(ref, octs, rows):
        return jnp.concatenate([wide(ref, at[q] + 2 * h, rows) for q in octs for h in range(2)], axis=1)

    for base, octs, source in ((0, (0, 1, 2, 3, 4), mine), (4, (1, 2, 3, 4), other)):
        for half in range(2):
            right = left(source, octs, pl.ds(256 * half, 256))
            value = lax.dot_general(left(mine, octs, every), right, NT, preferred_element_type=F32)
            put(near_ref, base, half, value)

    sources = {2: mine, 3: other}
    for base, q, octs in ((0, 0, (2,)), (4, 1, (2, 3)), (8, 4, (2, 3))):
        for half in range(2):
            right = jnp.concatenate(
                [wide(sources[o], at[q] + 2 * half, every) for o in octs], axis=0
            )
            value = jnp.dot(left(mine, octs, every), right, preferred_element_type=F32)
            put(part_ref, base, half, value)


def local(meta, density, mine, after):
    capacity = density.shape[1]
    return pl.pallas_call(
        local_kernel,
        grid_spec=pltpu.PrefetchScalarGridSpec(
            num_scalar_prefetch=1,
            grid=(1,),
            in_specs=[IN_HBM, pl.BlockSpec((24, 512, 128), lambda i, m: (0, 0, 0)), IN_HBM],
            out_specs=[pl.BlockSpec((n, 512, 128), lambda i, m: (0, 0, 0)) for n in (12, 8)],
            scratch_shapes=[
                pltpu.VMEM((8, capacity, 64, 64), BF),
                pltpu.SemaphoreType.DMA((8,)),
                pltpu.VMEM((24, 512, 128), BF),
            ],
        ),
        out_shape=[
            jax.ShapeDtypeStruct((12, 512, 128), F32),
            jax.ShapeDtypeStruct((8, 512, 128), BF),
        ],
        compiler_params=pltpu.CompilerParams(vmem_limit_bytes=54 << 20),
        cost_estimate=pl.CostEstimate(
            flops=4 << 30, bytes_accessed=16 << 20, transcendentals=0
        ),
        name="local",
    )(meta, density, mine, after)


def unfold(tiles_ref, full_ref):
    for n, (u, t) in enumerate(SYM):
        tile = tiles_ref[n]
        full_ref[t, 128 * u : 128 * u + 128, :] = tile
        if t > u:
            full_ref[u, 128 * t : 128 * t + 128, :] = tile.T


def sides(left, starts):
    every = pl.ds(0, 512)
    return jnp.concatenate([wide(left, p + 2 * h, every) for p in starts for h in range(2)], axis=1)


def most_kernel(meta, counts, left, part, near, ss, ms, corner, out_ref, first_ref, y, full):
    layer = lax.axis_index("layer")
    start = 16 * lax.axis_index("rows")
    at = [4 * octant(layer, q) for q in range(5)]
    step = pl.program_id(0)

    @pl.when(step == 0)
    def _():
        for q in range(2):
            for p in range(4):
                y[at[2 + q] + p] = near[4 * q + p]
        every = pl.ds(0, 512)

        def put(q, base, half, value):
            for s in range(2):
                p = 2 * half + s
                total = part[base + p] + value[:, 128 * s : 128 * s + 128]
                if q == 0:
                    first_ref[p] = total
                else:
                    y[at[q] + p] = total.astype(BF)

        unfold(corner, full)
        for half in range(2):
            right = wide(full, 2 * half, every)
            put(4, 8, half, jnp.dot(sides(left, at[4:5]), right, preferred_element_type=F32))
        unfold(ss, full)
        for half in range(2):
            top = jnp.concatenate(
                [
                    jnp.concatenate([ms[4 * u + 2 * half], ms[4 * u + 2 * half + 1]], axis=1)
                    for u in range(4)
                ],
                axis=0,
            )
            right = jnp.concatenate([top, wide(full, 2 * half, every)], axis=0)
            put(1, 4, half, jnp.dot(sides(left, at[0:2]), right, preferred_element_type=F32))
        for half in range(2):
            right = jnp.concatenate(
                [
                    jnp.concatenate([ms[4 * u + t] for t in range(4)], axis=1)
                    for u in (2 * half, 2 * half + 1)
                ],
                axis=0,
            )
            value = lax.dot_general(sides(left, at[1:2]), right, NT, preferred_element_type=F32)
            put(0, 0, half, value)

    for r in range(2):
        i = 2 * step + r
        k = 8 * layer + i
        count = counts[start + k]
        rows = pl.ds(pl.multiple_of(64 * i, 64), 64)
        for d in range(33):
            pair = 4 * layer + step + (r + d) // 2
            odd = (r + d) % 2
            slot = meta[k, d]
            block = y[pair, rows, :][:, 64 * odd : 64 * odd + 64]
            out_ref[r, slot] = jnp.where(slot < count, block, jnp.zeros_like(block))


def most(meta, counts, parts, tiles, capacity):
    def whole(n, rows):
        return pl.BlockSpec((n, rows, 128), lambda i, m, c: (0, 0, 0))

    return pl.pallas_call(
        most_kernel,
        grid_spec=pltpu.PrefetchScalarGridSpec(
            num_scalar_prefetch=2,
            grid=(4,),
            in_specs=[whole(24, 512), whole(12, 512), whole(8, 512)]
            + [whole(n, 128) for n in (10, 16, 10)],
            out_specs=[
                pl.BlockSpec((2, capacity, 64, 64), lambda i, m, c: (i, 0, 0, 0)),
                whole(4, 512),
            ],
            scratch_shapes=[
                pltpu.VMEM((24, 512, 128), BF),
                pltpu.VMEM((4, 512, 128), BF),
            ],
        ),
        out_shape=[
            jax.ShapeDtypeStruct((8, capacity, 64, 64), BF),
            jax.ShapeDtypeStruct((4, 512, 128), F32),
        ],
        compiler_params=pltpu.CompilerParams(vmem_limit_bytes=40 << 20),
        cost_estimate=pl.CostEstimate(
            flops=1 << 30, bytes_accessed=12 << 20, transcendentals=0
        ),
        name="most",
    )(meta, counts, *parts, *tiles)


def last_kernel(meta, counts, first, left, mm, _, out_ref, full, y, stage, sem):
    layer = lax.axis_index("layer")
    start = 16 * lax.axis_index("rows")
    unfold(mm, full)
    for half in range(2):
        right = wide(full, 2 * half, pl.ds(0, 512))
        value = jnp.dot(sides(left, (4 * octant(layer, 0),)), right, preferred_element_type=F32)
        for s in range(2):
            p = 2 * half + s
            y[p] = (first[p] + value[:, 128 * s : 128 * s + 128]).astype(BF)
    sign = 1 - 2 * layer
    base = jnp.where(layer == 0, 0, 32)
    for i in range(8):
        k = 8 * layer + i
        count = counts[start + k]
        for e in range(8):
            at = 8 * i + e

            @pl.when((e - i) * sign >= 0)
            def _():
                slot = meta[k, base + e - i]
                block = y[e // 2, 64 * i : 64 * i + 64, :][:, 64 * (e % 2) : 64 * (e % 2) + 64]
                stage[at] = jnp.where(slot < count, block, jnp.zeros_like(block))
                pltpu.make_async_copy(stage.at[at], out_ref.at[i, slot], sem).start()

    done = stage.at[pl.ds(0, 36)]
    pltpu.make_async_copy(done, done, sem).wait()


def last(meta, counts, first, left, mm, square):
    def whole(n, rows):
        return pl.BlockSpec((n, rows, 128), lambda i, m, c: (0, 0, 0))

    return pl.pallas_call(
        last_kernel,
        grid_spec=pltpu.PrefetchScalarGridSpec(
            num_scalar_prefetch=2,
            grid=(1,),
            in_specs=[whole(4, 512), whole(24, 512), whole(10, 128), IN_HBM],
            out_specs=IN_HBM,
            scratch_shapes=[
                pltpu.VMEM((4, 512, 128), BF),
                pltpu.VMEM((4, 512, 128), BF),
                pltpu.VMEM((64, 64, 64), BF),
                pltpu.SemaphoreType.DMA,
            ],
        ),
        out_shape=jax.ShapeDtypeStruct(square.shape, BF),
        input_output_aliases={5: 0},
        compiler_params=pltpu.CompilerParams(vmem_limit_bytes=16 << 20),
        cost_estimate=pl.CostEstimate(
            flops=1 << 28, bytes_accessed=3 << 20, transcendentals=0
        ),
        name="last",
    )(meta, counts, first, left, mm, square)


def totals_kernel(scale, sent, populations_ref, traces_ref):
    total = jnp.sum(sent[...], axis=0)[:, 0:64]
    populations_ref[...] = total[0:DOM_DEV]
    for n in range(2):
        traces_ref[n] = jnp.sum(total[DOM_DEV + n : DOM_DEV + n + 1]) * scale


def totals(gathered, scale):
    return pl.pallas_call(
        functools.partial(totals_kernel, scale),
        in_specs=[pl.BlockSpec(memory_space=pltpu.VMEM)],
        out_specs=[
            pl.BlockSpec(memory_space=pltpu.VMEM),
            pl.BlockSpec(memory_space=pltpu.SMEM),
        ],
        out_shape=[
            jax.ShapeDtypeStruct((DOM_DEV, 64), F32),
            jax.ShapeDtypeStruct((2,), F32),
        ],
        compiler_params=pltpu.CompilerParams(vmem_limit_bytes=16 << 20),
        name="totals",
    )(gathered)


def per_device(density, col_index, counts, domain):
    per_dev, capacity, width = density.shape[:3]
    block_rows = col_index.shape[0]
    radius = (capacity - 1) // 2
    slabs = lax.axis_size("rows")
    devices = slabs * lax.axis_size("layer")
    start = lax.axis_index("rows") * per_dev

    columns = lax.dynamic_slice_in_dim(col_index.T, start, per_dev, 1)
    row_ids = start + jnp.arange(per_dev, dtype=jnp.int32)
    offset = (columns - row_ids[None, :] + radius) % block_rows
    lane = jnp.arange(40, dtype=jnp.int32)
    slots = jnp.arange(capacity, dtype=jnp.int32)
    meta = jnp.sum(
        jnp.where(offset.T[:, :, None] == lane[None, None, :], slots[None, :, None], 0), axis=1
    )

    def device(row, core):
        return (row % slabs) * 2 + core

    ahead = [(device(r, 0), device(r + 1, 0)) for r in range(slabs)]
    ahead += [(device(r, 1), device(r - 1, 1)) for r in range(slabs)]
    across = [(device(r, c), device(r, 1 - c)) for r in range(slabs) for c in range(2)]

    (ss,) = pack(((SYM, 1, 1),), meta, density)
    ms, mm = pack(((FULL, 0, 1), (SYM, 0, 0)), meta, density, ss)
    partial, mine = diagonals(meta, domain, density, mm, devices)
    ss = lax.ppermute(ss, AXES, ahead)
    ms = lax.ppermute(ms, AXES, ahead)
    mm = lax.ppermute(mm, AXES, ahead)
    gathered = lax.all_to_all(partial, AXES, 0, 0, tiled=True)
    part, near = local(meta, density, mine, partial)
    corner = lax.ppermute(ss, AXES, across)
    square, first = most(meta, counts, (mine, part, near), (ss, ms, corner), capacity)
    square = last(meta, counts, first, mine, mm, square)

    populations, traces = totals(gathered, 1.0 / (block_rows * width))
    return (square, populations, traces)


def solution(mesh):
    placed = (P("rows", None, None, None), P(), P(), P())
    return jax.shard_map(
        per_device,
        mesh=mesh,
        in_specs=placed,
        out_specs=(P(("rows", "layer"), None, None, None), P(("rows", "layer"), None), P()),
        check_vma=False,
    )
```

time: 913 us -> 52.5 us (0.06)
  waiting for transfers between devices: 344 us -> 0.01 us
  matrix products: 262 us -> 0 us
  local copies, waits for them, and re-layouts: 225 us -> 3.12 us
  blocking collectives: 40.2 us -> 0 us
  Pallas kernels: 0 us -> 35.1 us
  other arithmetic: 27.2 us -> 1.55 us
    ppermute x2 -> x4, waiting for transfers between devices: 344 us -> 0.01 us  [the longest x1 0.01 us: per_device(): ms = lax.ppermute(ms, AXES, ahead)]
    dot_general x17 -> x0, matrix products: 262 us -> none  [the longest x8 173 us: row_block(): jnp.einsum('amb,abxy->amxy', select.astype(jnp.bfloat16), partner_rows, p...]
    gather x45 -> x0, local copies, waits for them, and re-layouts: 163 us -> none  [the longest x8 129 us: row_block(): partner_rows = banded[position]]
    unnamed x1 -> x0, blocking collectives: 40.2 us -> none
    pallas_call x0 -> x7, Pallas kernels: none -> 35.1 us  [the longest x1 10.9 us: local(): pl.pallas_call(local_kernel, grid_spec=pltpu.PrefetchScalarGridSpec(num_s...]
    unnamed x20 -> x10, local copies, waits for them, and re-layouts: 22.2 us -> 3.12 us
    concatenate x2 -> x0, other arithmetic: 18.6 us -> none  [the longest x1 18.6 us: padded(): value = jnp.concatenate([before, value, after], axis=dim)]
    while x1 -> x0, local copies, waits for them, and re-layouts: 15.7 us -> none  [per_device(): lax.map(lambda local: row_block(layer_id * half_rows + local, slot_ids),...]
  transfers between devices with their start and end apart: 2 -> 5, of which waited for: 2 -> 0; matrix products, arithmetic and copies ran while one was open for 3% -> 0% of each run, Pallas kernels for 0% -> 54%
where the time goes in v1:
time: 52.5 us; the launch traced here: 51.7 us
  Pallas kernels  35.1 us (67%)
  starting transfers between devices  11.2 us (21%)
  local copies, waits for them, and re-layouts  3.12 us (6%)
  other arithmetic  1.55 us (3%)
  between operations  0.76 us (1%)
    pallas_call x1, Pallas kernels, local(): pl.pallas_call(local_kernel, grid_spec=pltpu.PrefetchScalarGridSpec(num_s...  10.9 us
    pallas_call x1, Pallas kernels, diagonals(): pl.pallas_call(diag_kernel, grid_spec=pltpu.PrefetchScalarGridSpec(num_sc...  6.74 us
    pallas_call x1, Pallas kernels, most(): pl.pallas_call(most_kernel, grid_spec=pltpu.PrefetchScalarGridSpec(num_sc...  6.41 us
    pallas_call x2, Pallas kernels, pack(): pl.pallas_call(functools.partial(pack_kernel, groups), grid_spec=pltpu.Pr...  5.9 us
    all_to_all x1, starting transfers between devices, per_device(): gathered = lax.all_to_all(partial, AXES, 0, 0, tiled=True)  4.84 us
    pallas_call x1, Pallas kernels, last(): pl.pallas_call(last_kernel, grid_spec=pltpu.PrefetchScalarGridSpec(num_sc...  4.44 us
    unnamed x10, local copies, waits for them, and re-layouts  3.12 us
    ppermute x1, starting transfers between devices, per_device(): ss = lax.ppermute(ss, AXES, ahead)  3.02 us
  transfers between devices with their start and end apart: 5, of which 0 were waited for; matrix products, arithmetic and copies ran while one was open for 0% of the time, Pallas kernels for 54%

profile of v1, /device:TPU:0, one launch (start us, length us, event | category | flops | bytes accessed | tf_op | source)
XLA Modules:
  0.0 51.7 jit_solution(3246340993135043619)
XLA Ops:
  0.6 0.8 %add_select_fusion = s32[16,33]{0,1:T(8,128)S(1)} fusion(s32[256,33]{0,1:T(8,128)} %param.5, s32[]{:T(128)S(6)} %select_n.15, s32[16]{0:T(128)S(1)} %iota_add_fusion), kind=kLoop, calls=%fused_computation.2 | loop fusion | flops 6864 | bytes 4292 | tf_op jit(solution)/shard_map/jit(remainder)/select_n | solution.py:440
  1.5 0.7 %select_reduce_fusion.meta = s32[16,40]{1,0:T(8,128)} fusion(s32[16,33]{0,1:T(8,128)S(1)} %add_select_fusion), kind=kLoop, calls=%fused_computation | loop fusion | flops 62720 | bytes 4672 | tf_op jit(solution)/shard_map/reduce_sum | solution.py:443
  2.2 2.7 %pack.2.rest_0_ = bf16[10,128,128]{2,1,0:T(8,128)(2,1)} custom-call(s32[16,40]{1,0:T(8,128)} %select_reduce_fusion.meta, bf16[16,33,64,64]{3,2,1,0:T(8,128)(2,1)} %density.5), custom_call_target="tpu_custom_call" | custom-call | bytes 1310720 | tf_op jit(solution)/shard_map/pack/pallas_call | solution.py:50
  4.9 3.0 %collective-permute-start = (bf16[10,128,128]{2,1,0:T(8,128)(2,1)}, bf16[10,128,128]{2,1,0:T(8,128)(2,1)}, u32[]{:S(2)}, u32[]{:S(2)}) collective-permute-start(bf16[10,128,128]{2,1,0:T(8,128)(2,1)} %pack.2.rest_0_), channel_id=1, source_target_pairs={{0,2},{2,4},{4,6},{6,8},{8,10},{10,12},{12,14},{14,16},{16,18},{18... | collective-permute-start | bytes 983048 | tf_op jit(solution)/shard_map/ppermute | solution.py:457
  7.9 3.2 %pack.3 = (bf16[16,128,128]{2,1,0:T(8,128)(2,1)}, bf16[10,128,128]{2,1,0:T(8,128)(2,1)}) custom-call(s32[16,40]{1,0:T(8,128)} %select_reduce_fusion.meta, bf16[16,33,64,64]{3,2,1,0:T(8,128)(2,1)} %density.5, bf16[10,128,128]{2,1,0:T(8,128)(2,1)} %pack.2.rest_0_), custom_call_target="tpu_custom_call" | custom-call | bytes 3407872 | tf_op jit(solution)/shard_map/pack/pallas_call | solution.py:50
  11.1 1.5 %collective-permute-start.1 = (bf16[16,128,128]{2,1,0:T(8,128)(2,1)}, bf16[16,128,128]{2,1,0:T(8,128)(2,1)}, u32[]{:S(2)}, u32[]{:S(2)}) collective-permute-start(bf16[16,128,128]{2,1,0:T(8,128)(2,1)} %get-tuple-element.18), channel_id=1, source_target_pairs={{0,2},{2,4},{4,6},{6,8},{8,10},{10,12},{12,14},{14,16},{16,18},{18... | collective-permute-start | bytes 1572872 | tf_op jit(solution)/shard_map/ppermute | solution.py:458
  12.7 1.5 %collective-permute-start.3 = (bf16[10,128,128]{2,1,0:T(8,128)(2,1)}, bf16[10,128,128]{2,1,0:T(8,128)(2,1)}, u32[]{:S(2)}, u32[]{:S(2)}) collective-permute-start(bf16[10,128,128]{2,1,0:T(8,128)(2,1)} %get-tuple-element.13._), channel_id=1, source_target_pairs={{0,2},{2,4},{4,6},{6,8},{8,10},{10,12},{12,14},{14,16},{16,18},{18... | collective-permute-start | bytes 983048 | tf_op jit(solution)/shard_map/ppermute | solution.py:459
  14.2 6.7 %diagonals.1 = (f32[32,8,128]{2,1,0:T(8,128)}, bf16[24,512,128]{2,1,0:T(8,128)(2,1)}) custom-call(s32[16,40]{1,0:T(8,128)} %select_reduce_fusion.meta, s32[256]{0:T(256)} %domain.1, bf16[16,33,64,64]{3,2,1,0:T(8,128)(2,1)} %density.5, bf16[10,128,128]{2,1,0:T(8,128)(2,1)} %get-tuple-element.13._), custom_call_target="tpu_custom_call" | custom-call | bytes 8388608 | tf_op jit(solution)/shard_map/diagonals/pallas_call | solution.py:132
  20.9 4.8 %all-to-all-start = ((f32[32,8,128]{2,1,0:T(8,128)}), f32[32,8,128]{2,1,0:T(8,128)S(1)}, u32[]{:S(2)}, u32[]{:S(2)}) async-start(f32[32,8,128]{2,1,0:T(8,128)} %get-tuple-element.15._), calls=%async_computation | async-start | bytes 262144 | tf_op jit(solution)/shard_map/all_to_all | solution.py:460
  25.8 0.0 collective-permute-done.ss
  25.8 0.3 collective-permute-start.2
  26.1 10.9 %local.1 = (f32[12,512,128]{2,1,0:T(8,128)}, bf16[8,512,128]{2,1,0:T(8,128)(2,1)}) custom-call(s32[16,40]{1,0:T(8,128)} %select_reduce_fusion.meta, bf16[16,33,64,64]{3,2,1,0:T(8,128)(2,1)} %density.5, bf16[24,512,128]{2,1,0:T(8,128)(2,1)} %get-tuple-element.14.mine.left, f32[32,8,128]{2,1,0:T(8,128)} %get-tuple-element.15._), custom_call_target="tpu_custom_call" | custom-call | flops 4294967296 | bytes 16777216 | tf_op jit(solution)/shard_map/local/pallas_call | solution.py:218
  37.0 0.0 all-to-all-done.sent
  37.0 0.7 %totals.1 = (f32[2,64]{1,0:T(2,128)}, f32[2]{0:T(128)}) custom-call(f32[32,8,128]{2,1,0:T(8,128)S(1)} %all-to-all-done.sent), custom_call_target="tpu_custom_call" | custom-call | tf_op jit(solution)/shard_map/totals/pallas_call | solution.py:414
  37.7 0.0 collective-permute-done.1.ms
  37.7 0.0 collective-permute-done.2.corner
  37.7 0.0 copy-done
  37.8 0.0 copy-done.3
  37.8 0.0 copy-done.4
  37.8 1.9 %copy-done.1 = f32[12,512,128]{2,1,0:T(8,128)S(1)} copy-done((f32[12,512,128]{2,1,0:T(8,128)S(1)}, f32[12,512,128]{2,1,0:T(8,128)}, u32[]{:S(2)}) %copy-start.1) | copy-done | bytes 3145752
  39.7 1.2 %copy-done.2 = bf16[8,512,128]{2,1,0:T(8,128)(2,1)S(1)} copy-done((bf16[8,512,128]{2,1,0:T(8,128)(2,1)S(1)}, bf16[8,512,128]{2,1,0:T(8,128)(2,1)}, u32[]{:S(2)}) %copy-start.2) | copy-done | bytes 1048600
  40.9 6.4 %most.1 = (bf16[8,33,64,64]{3,2,1,0:T(8,128)(2,1)}, f32[4,512,128]{2,1,0:T(8,128)S(1)}) custom-call(s32[16,40]{1,0:T(8,128)S(1)} %copy-done.3, s32[256]{0:T(256)S(1)} %copy-done.4, bf16[24,512,128]{2,1,0:T(8,128)(2,1)S(1)} %copy-done, f32[12,512,128]{2,1,0:T(8,128)S(1)} %copy-done.1, bf16[8,512,128]{2,1,0:T(8,128)(2,1)S(1)} %copy-done.2, ...), custom_call_target="tpu_custom_call" | custom-call | flops 1073741824 | bytes 12582912 | tf_op jit(solution)/shard_map/most/pallas_call | solution.py:321
  47.3 0.0 collective-permute-done.3.mm
  47.3 4.4 %last.1 = bf16[8,33,64,64]{3,2,1,0:T(8,128)(2,1)} custom-call(s32[16,40]{1,0:T(8,128)S(1)} %copy-done.3, s32[256]{0:T(256)S(1)} %copy-done.4, f32[4,512,128]{2,1,0:T(8,128)S(1)} %get-tuple-element.19.first, bf16[24,512,128]{2,1,0:T(8,128)(2,1)S(1)} %copy-done, bf16[10,128,128]{2,1,0:T(8,128)(2,1)} %collective-permute-done.3.mm, ...), custom_call_target="tpu_custom_call", output_to_operand_aliasing={{}: (5, {})} | custom-call | flops 268435456 | bytes 3145728 | tf_op jit(solution)/shard_map/last/pallas_call | solution.py:382
  (6 shorter events, 0.0 us)
Async XLA Ops:
  4.9 20.8 %collective-permute-start = (bf16[10,128,128]{2,1,0:T(8,128)(2,1)}, bf16[10,128,128]{2,1,0:T(8,128)(2,1)}, u32[]{:S(2)}, u32[]{:S(2)}) collective-permute-start(bf16[10,128,128]{2,1,0:T(8,128)(2,1)} %pack.2.rest_0_), channel_id=1, source_target_pairs={{0,2},{2,4},{4,6},{6,8},{8,10},{10,12},{12,14},{14,16},{16,18},{18... | collective-permute-start | bytes 983048 | tf_op jit(solution)/shard_map/ppermute | solution.py:457
  11.1 26.6 %collective-permute-start.1 = (bf16[16,128,128]{2,1,0:T(8,128)(2,1)}, bf16[16,128,128]{2,1,0:T(8,128)(2,1)}, u32[]{:S(2)}, u32[]{:S(2)}) collective-permute-start(bf16[16,128,128]{2,1,0:T(8,128)(2,1)} %get-tuple-element.18), channel_id=1, source_target_pairs={{0,2},{2,4},{4,6},{6,8},{8,10},{10,12},{12,14},{14,16},{16,18},{18... | collective-permute-start | bytes 1572872 | tf_op jit(solution)/shard_map/ppermute | solution.py:458
  12.7 34.6 %collective-permute-start.3 = (bf16[10,128,128]{2,1,0:T(8,128)(2,1)}, bf16[10,128,128]{2,1,0:T(8,128)(2,1)}, u32[]{:S(2)}, u32[]{:S(2)}) collective-permute-start(bf16[10,128,128]{2,1,0:T(8,128)(2,1)} %get-tuple-element.13._), channel_id=1, source_target_pairs={{0,2},{2,4},{4,6},{6,8},{8,10},{10,12},{12,14},{14,16},{16,18},{18... | collective-permute-start | bytes 983048 | tf_op jit(solution)/shard_map/ppermute | solution.py:459
  20.9 16.1 %all-to-all-start = ((f32[32,8,128]{2,1,0:T(8,128)}), f32[32,8,128]{2,1,0:T(8,128)S(1)}, u32[]{:S(2)}, u32[]{:S(2)}) async-start(f32[32,8,128]{2,1,0:T(8,128)} %get-tuple-element.15._), calls=%async_computation | async-start | bytes 262144 | tf_op jit(solution)/shard_map/all_to_all | solution.py:460
  25.8 12.0 %collective-permute-start.2 = (bf16[10,128,128]{2,1,0:T(8,128)(2,1)}, bf16[10,128,128]{2,1,0:T(8,128)(2,1)}, u32[]{:S(2)}, u32[]{:S(2)}) collective-permute-start(bf16[10,128,128]{2,1,0:T(8,128)(2,1)} %collective-permute-done.ss), channel_id=1, source_target_pairs={{0,1},{1,0},{2,3},{3,2},{4,5},{5,4},{6,7},{7,6},{8,9},{9,8},{10,11... | collective-permute-start | bytes 983048 | tf_op jit(solution)/shard_map/ppermute | solution.py:462
  26.1 11.7 %copy-start = (bf16[24,512,128]{2,1,0:T(8,128)(2,1)S(1)}, bf16[24,512,128]{2,1,0:T(8,128)(2,1)}, u32[]{:S(2)}) copy-start(bf16[24,512,128]{2,1,0:T(8,128)(2,1)} %get-tuple-element.14.mine.left) | copy-start | bytes 9437188
  26.1 11.7 %copy-start.3 = (s32[16,40]{1,0:T(8,128)S(1)}, s32[16,40]{1,0:T(8,128)}, u32[]{:S(2)}) copy-start(s32[16,40]{1,0:T(8,128)} %select_reduce_fusion.meta) | copy-start | bytes 7684
  26.1 11.7 %copy-start.4 = (s32[256]{0:T(256)S(1)}, s32[256]{0:T(256)}, u32[]{:S(2)}) copy-start(s32[256]{0:T(256)} %counts.3) | copy-start | bytes 3076
  37.8 1.9 %copy-start.1 = (f32[12,512,128]{2,1,0:T(8,128)S(1)}, f32[12,512,128]{2,1,0:T(8,128)}, u32[]{:S(2)}) copy-start(f32[12,512,128]{2,1,0:T(8,128)} %get-tuple-element.16.part) | copy-start | bytes 9437188
  39.7 1.2 %copy-start.2 = (bf16[8,512,128]{2,1,0:T(8,128)(2,1)S(1)}, bf16[8,512,128]{2,1,0:T(8,128)(2,1)}, u32[]{:S(2)}) copy-start(bf16[8,512,128]{2,1,0:T(8,128)(2,1)} %get-tuple-element.17.near) | copy-start | bytes 3145732

commit v2 on v0

v2 whole, which is shorter than its diff:
```python
import functools

import jax
import jax.numpy as jnp
from jax import lax
from jax.experimental import pallas as pl
from jax.experimental.pallas import tpu as pltpu
from jax.sharding import PartitionSpec as P


DOM_DEV = 2
AXES = ("rows", "layer")
SYM = [(u, t) for u in range(4) for t in range(u, 4)]
FULL = [(u, t) for u in range(4) for t in range(4)]
NT = (((1,), (1,)), ((), ()))
BF = jnp.bfloat16
F32 = jnp.float32
EVERY = pl.ds(0, 512)
IN_HBM = pl.BlockSpec(memory_space=pltpu.HBM)


def issue(groups, meta, density, buf, sems):
    layer = lax.axis_index("layer")
    starts = (8 * layer, 8 * (1 - layer))
    base = 0
    for g, (tiles, near, far) in enumerate(groups):
        row, col = starts[near], starts[far]
        for n, (u, t) in enumerate(tiles):
            for r in range(2):
                for s in range(2):
                    k = row + 2 * u + r
                    slot = meta[k, (col - row) + 2 * t + s - 2 * u - r + 16]
                    at = base + 4 * n + 2 * r + s
                    pltpu.make_async_copy(density.at[k, slot], buf.at[at], sems.at[g]).start()
        base += 4 * len(tiles)


def collect(groups, outs, buf, sems):
    base = 0
    for g, (tiles, _, _) in enumerate(groups):
        span = buf.at[pl.ds(base, 4 * len(tiles))]
        pltpu.make_async_copy(span, span, sems.at[g]).wait()
        for n in range(len(tiles)):
            for r in range(2):
                at = base + 4 * n + 2 * r
                outs[g][n, 64 * r : 64 * r + 64, :] = jnp.concatenate(
                    [buf[at], buf[at + 1]], axis=1
                )
        base += 4 * len(tiles)


def pack_kernel(groups, meta, density, *rest):
    outs, buf, sems = rest[: len(groups)], rest[-2], rest[-1]
    issue(groups, meta, density, buf, sems)
    collect(groups, outs, buf, sems)


def pack(groups, meta, density):
    sizes = [len(tiles) for tiles, _, _ in groups]
    return pl.pallas_call(
        functools.partial(pack_kernel, groups),
        grid_spec=pltpu.PrefetchScalarGridSpec(
            num_scalar_prefetch=1,
            grid=(1,),
            in_specs=[IN_HBM],
            out_specs=[pl.BlockSpec((n, 128, 128), lambda i, m: (0, 0, 0)) for n in sizes],
            scratch_shapes=[
                pltpu.VMEM((4 * sum(sizes), 64, 64), BF),
                pltpu.SemaphoreType.DMA((len(sizes),)),
            ],
        ),
        out_shape=[jax.ShapeDtypeStruct((n, 128, 128), BF) for n in sizes],
        compiler_params=pltpu.CompilerParams(vmem_limit_bytes=16 << 20),
        cost_estimate=pl.CostEstimate(
            flops=0, bytes_accessed=sum(sizes) << 17, transcendentals=0
        ),
        name="pack",
    )(meta, density)


def rest_kernel(groups, meta, domain, density, _, *rest):
    outs, out_ref = rest[: len(groups)], rest[len(groups)]
    buf, packed, rows_ref, sems, sums = rest[len(groups) + 1 :]
    layer = lax.axis_index("layer")
    start = 16 * lax.axis_index("rows")
    base = 8 * layer
    issue(groups, meta, density, buf, packed)
    for i in range(4):
        source = density.at[pl.ds(base + 2 * i, 2)]
        pltpu.make_async_copy(source, rows_ref.at[pl.ds(2 * i, 2)], sems.at[i]).start()
    out_ref[...] = jnp.zeros_like(out_ref)
    sums[...] = jnp.zeros_like(sums)
    eye = lax.broadcasted_iota(jnp.int32, (64, 64), 0) == lax.broadcasted_iota(
        jnp.int32, (64, 64), 1
    )
    sub = lax.broadcasted_iota(jnp.int32, (8, 64), 0)
    collect(groups, outs, buf, packed)

    @pl.loop(0, 4)
    def _(u):
        pltpu.make_async_copy(
            density.at[pl.ds(0, 2)], rows_ref.at[pl.ds(2 * u, 2)], sems.at[u]
        ).wait()
        for r in range(2):
            i = 2 * u + r
            k = base + i
            total = jnp.zeros((64, 64), F32)
            for s in range(rows_ref.shape[1]):
                block = rows_ref[i, s].astype(F32)
                total += block * block
            column = jnp.sum(total, axis=1, keepdims=True)
            squares = jnp.sum(jnp.where(eye, column, 0.0), axis=0, keepdims=True)
            squares = squares.astype(BF).astype(F32)
            middle = rows_ref[i, meta[k, 16]].astype(F32)
            diagonal = jnp.sum(jnp.where(eye, middle, 0.0), axis=0, keepdims=True)
            target = domain[start + k]
            owner = target // DOM_DEV
            place = target - owner * DOM_DEV
            out_ref[owner, :, 0:64] = out_ref[owner, :, 0:64] + jnp.where(
                sub == place, squares, 0.0
            )
            sums[:, 0:64] = sums[:, 0:64] + jnp.where(
                sub == DOM_DEV, diagonal, jnp.where(sub == DOM_DEV + 1, squares, 0.0)
            )

    out_ref[...] = out_ref[...] + sums[...][None]


def rest(groups, meta, domain, density, after, devices):
    capacity = density.shape[1]
    sizes = [len(tiles) for tiles, _, _ in groups]
    shapes = [(n, 128, 128) for n in sizes] + [(devices, 8, 128)]
    return pl.pallas_call(
        functools.partial(rest_kernel, groups),
        grid_spec=pltpu.PrefetchScalarGridSpec(
            num_scalar_prefetch=2,
            grid=(1,),
            in_specs=[IN_HBM, IN_HBM],
            out_specs=[pl.BlockSpec(shape, lambda i, m, d: (0, 0, 0)) for shape in shapes],
            scratch_shapes=[
                pltpu.VMEM((4 * sum(sizes), 64, 64), BF),
                pltpu.SemaphoreType.DMA((len(sizes),)),
                pltpu.VMEM((8, capacity, 64, 64), BF),
                pltpu.SemaphoreType.DMA((4,)),
                pltpu.VMEM((8, 128), F32),
            ],
        ),
        out_shape=[
            jax.ShapeDtypeStruct(shape, F32 if n == len(sizes) else BF)
            for n, shape in enumerate(shapes)
        ],
        compiler_params=pltpu.CompilerParams(vmem_limit_bytes=16 << 20),
        cost_estimate=pl.CostEstimate(flops=0, bytes_accessed=8 << 20, transcendentals=0),
        name="rest",
    )(meta, domain, density, after)


def spread(slots, block, own, first, at, k):
    zero = jnp.zeros((64, 64), BF)
    for r in range(2):
        rows = pl.ds(pl.multiple_of(at + 64 * r, 64), 64)
        for pp in range(17):
            halves = []
            for s in range(2):
                d = 2 * pp + s - r
                halves.append(block(r, slots[k + r, d]) if 0 <= d <= 32 else zero)
            own[first + pp, rows, :] = jnp.concatenate(halves, axis=1)


def octant(layer, q):
    return jnp.where(layer == 0, q, 5 - q)


def wide(ref, pair, rows):
    return jnp.concatenate([ref[pair, rows, :], ref[pair + 1, rows, :]], axis=1)


def local_kernel(meta, counts, density, _, head_ref, rest_ref, part_ref, out_ref, *scratch):
    rows_ref, sems, mine, other, near_ref, stage, sent = scratch
    layer = lax.axis_index("layer")
    base = 8 * layer
    sib = 8 * (1 - layer)
    for n in range(8):
        source = density.at[pl.ds((base if n < 4 else sib) + 2 * (n % 4), 2)]
        pltpu.make_async_copy(source, rows_ref.at[pl.ds(2 * n, 2)], sems.at[n]).start()

    @pl.loop(0, 24)
    def _(p):
        mine[p] = jnp.zeros(mine.shape[1:], BF)
        other[p] = jnp.zeros(other.shape[1:], BF)

    def gather(u, own, first, at, k):
        pltpu.make_async_copy(
            density.at[pl.ds(0, 2)], rows_ref.at[pl.ds(2 * u, 2)], sems.at[u]
        ).wait()
        spread(meta, lambda r, slot: rows_ref[2 * u + r, slot], own, first, at, k)

    @pl.loop(0, 4)
    def _(u):
        gather(u, mine, 4 * layer + u, 128 * u, base + 2 * u)

    at = [4 * octant(layer, q) for q in range(5)]
    every = pl.ds(0, 512)

    def put(ref, base, half, value):
        ref[base + 2 * half] = value[:, 0:128].astype(ref.dtype)
        ref[base + 2 * half + 1] = value[:, 128:256].astype(ref.dtype)

    def left(ref, octs, rows):
        return jnp.concatenate(
            [wide(ref, at[q] + 2 * h, rows) for q in octs for h in range(2)], axis=1
        )

    def own(base, octs, source):
        for half in range(2):
            right = left(source, octs, pl.ds(256 * half, 256))
            value = lax.dot_general(left(mine, octs, every), right, NT, preferred_element_type=F32)
            put(near_ref, base, half, value)

    def toward(ref, base, q, octs):
        for half in range(2):
            right = jnp.concatenate(
                [wide((mine, other)[o - 2], at[q] + 2 * half, every) for o in octs], axis=0
            )
            value = jnp.dot(left(mine, octs, every), right, preferred_element_type=F32)
            put(ref, base, half, value)

    for p in range(4):
        head_ref[p] = mine[at[0] + p]
        rest_ref[p] = mine[at[1] + p]
        rest_ref[4 + p] = mine[at[4] + p]

    def emit(base, first):
        for i in range(8):
            for e in range(8):
                n = 8 * base + 8 * i + e
                block = lane_half(near_ref, base // 2 + e // 2, pl.ds(64 * i, 64), e % 2)
                place_block(meta, counts, i, first + e, block, stage.at[n], out_ref, sent)

    own(0, (0, 1, 2, 3, 4), mine)
    emit(0, 16)
    toward(part_ref, 0, 0, (2,))

    @pl.loop(0, 4)
    def _(u):
        gather(u + 4, other, 4 * (1 - layer) + u, 128 * u, sib + 2 * u)

    own(4, (1, 2, 3, 4), other)
    emit(8, jnp.where(layer == 0, 24, 8))
    toward(part_ref, 4, 1, (2, 3))
    toward(part_ref, 8, 4, (2, 3))
    pltpu.make_async_copy(stage, stage, sent).wait()


def whole(*shape):
    return pl.BlockSpec(shape, lambda i, m, c: (0, 0, 0))


def local(meta, counts, density, after):
    capacity = density.shape[1]
    parts = ((4, BF), (8, BF), (12, F32))
    return pl.pallas_call(
        local_kernel,
        grid_spec=pltpu.PrefetchScalarGridSpec(
            num_scalar_prefetch=2,
            grid=(1,),
            in_specs=[IN_HBM, IN_HBM],
            out_specs=[whole(n, 512, 128) for n, _ in parts] + [IN_HBM],
            scratch_shapes=[
                pltpu.VMEM((16, capacity, 64, 64), BF),
                pltpu.SemaphoreType.DMA((8,)),
                pltpu.VMEM((24, 512, 128), BF),
                pltpu.VMEM((24, 512, 128), BF),
                pltpu.VMEM((8, 512, 128), BF),
                pltpu.VMEM((128, 64, 64), BF),
                pltpu.SemaphoreType.DMA,
            ],
        ),
        out_shape=[jax.ShapeDtypeStruct((n, 512, 128), t) for n, t in parts]
        + [jax.ShapeDtypeStruct((8, capacity, 64, 64), BF)],
        compiler_params=pltpu.CompilerParams(vmem_limit_bytes=36 << 20),
        cost_estimate=pl.CostEstimate(
            flops=4 << 30, bytes_accessed=16 << 20, transcendentals=0
        ),
        name="local",
    )(meta, counts, density, after)


def beside(tiles, base, count):
    return jnp.concatenate([tiles[base + n] for n in range(count)], axis=1)


def corners(tiles_ref):
    tile = {ut: tiles_ref[n] for n, ut in enumerate(SYM)}

    def square(u):
        top = jnp.concatenate([tile[u, u], tile[u, u + 1]], axis=1)
        bottom = jnp.concatenate([tile[u, u + 1].T, tile[u + 1, u + 1]], axis=1)
        return jnp.concatenate([top, bottom], axis=0)

    cross = jnp.concatenate(
        [jnp.concatenate([tile[u, 2], tile[u, 3]], axis=1) for u in range(2)], axis=0
    )
    return square(0), cross, square(2)


def product(ref, base, tiles_ref):
    upper, cross, lower = corners(tiles_ref)
    low, high = wide(ref, base, EVERY), wide(ref, base + 2, EVERY)
    yield 0, jnp.dot(low, upper, preferred_element_type=F32) + lax.dot_general(
        high, cross, NT, preferred_element_type=F32
    )
    yield 1, jnp.dot(
        jnp.concatenate([low, high], axis=1),
        jnp.concatenate([cross, lower], axis=0),
        preferred_element_type=F32,
    )


def lane_half(ref, pair, rows, odd):
    return ref[pair, rows, :][:, 64 * odd : 64 * odd + 64]


def place_block(meta, counts, i, c, block, stage, out_ref, sem):
    k = 8 * lax.axis_index("layer") + i
    slot = meta[k, c - i]
    live = slot < counts[16 * lax.axis_index("rows") + k]
    stage[...] = jnp.where(live, block, jnp.zeros_like(block))
    pltpu.make_async_copy(stage, out_ref.at[i, slot], sem).start()


def finish(ref, at, partial, base, half, value):
    for s in range(2):
        p = 2 * half + s
        total = partial[base + p] + value[:, 128 * s : 128 * s + 128]
        ref[at + p] = total.astype(ref.dtype)


def emit_edge(core, near, meta, counts, ref, stage, at, out_ref, sem):
    above = near == (core == 1)
    n = at
    for i in range(8):
        for e in range(i, 8) if above else range(i + 1):
            block = lane_half(ref, e // 2, pl.ds(64 * i, 64), e % 2)
            c = e if above else 32 + e
            place_block(meta, counts, i, c, block, stage.at[n], out_ref, sem)
            n += 1


def middle_kernel(
    meta, counts, head, others, part, ss, ms, corner, _, first_ref, out_ref, y, middle, stage, sem
):
    layer = lax.axis_index("layer")
    upper, cross, lower = corners(ss)
    high = jnp.concatenate([wide(others, 0, EVERY), wide(others, 2, EVERY)], axis=1)
    low = jnp.concatenate([wide(head, 0, EVERY), wide(head, 2, EVERY)], axis=1)
    for half in range(2):
        top = jnp.concatenate([beside(ms, 4 * u + 2 * half, 2) for u in range(4)], axis=0)
        value = jnp.dot(low, top, preferred_element_type=F32)
        if half:
            right = jnp.concatenate([cross, lower], axis=0)
            value += jnp.dot(high, right, preferred_element_type=F32)
        else:
            value += jnp.dot(high[:, 0:256], upper, preferred_element_type=F32)
            value += lax.dot_general(high[:, 256:512], cross, NT, preferred_element_type=F32)
        finish(middle, 0, part, 4, half, value)

    for i in range(8):
        for e in range(8):
            block = lane_half(middle, e // 2, pl.ds(64 * i, 64), e % 2)
            c = jnp.where(layer == 0, 8, 24) + e
            place_block(meta, counts, i, c, block, stage.at[8 * i + e], out_ref, sem)

    for half, value in product(others, 4, corner):
        finish(y, 0, part, 8, half, value)
    for core in range(2):
        pl.when(layer == core)(
            lambda core=core: emit_edge(core, True, meta, counts, y, stage, 64, out_ref, sem)
        )
    for half in range(2):
        right = jnp.concatenate([beside(ms, 4 * u, 4) for u in (2 * half, 2 * half + 1)], axis=0)
        value = lax.dot_general(high, right, NT, preferred_element_type=F32)
        finish(first_ref, 0, part, 0, half, value)
    pltpu.make_async_copy(stage, stage, sem).wait()


def last_kernel(meta, counts, head, first, mm, _, out_ref, y, stage, sem):
    layer = lax.axis_index("layer")
    for half, value in product(head, 0, mm):
        finish(y, 0, first, 0, half, value)
    for core in range(2):
        pl.when(layer == core)(
            lambda core=core: emit_edge(core, False, meta, counts, y, stage, 0, out_ref, sem)
        )
    pltpu.make_async_copy(stage, stage, sem).wait()


def closing(kernel, meta, counts, inputs, square, blocks, extra, buffers, limit):
    scratch = [pltpu.VMEM((4, 512, 128), BF)] * buffers
    return pl.pallas_call(
        kernel,
        grid_spec=pltpu.PrefetchScalarGridSpec(
            num_scalar_prefetch=2,
            grid=(1,),
            in_specs=[whole(*x.shape) for x in inputs] + [IN_HBM],
            out_specs=[whole(*x.shape) for x in extra] + [IN_HBM],
            scratch_shapes=scratch + [pltpu.VMEM((blocks, 64, 64), BF), pltpu.SemaphoreType.DMA],
        ),
        out_shape=[*extra, jax.ShapeDtypeStruct(square.shape, BF)],
        input_output_aliases={2 + len(inputs): len(extra)},
        compiler_params=pltpu.CompilerParams(vmem_limit_bytes=limit << 20),
        cost_estimate=pl.CostEstimate(
            flops=len(inputs) << 27, bytes_accessed=6 << 20, transcendentals=0
        ),
    )(meta, counts, *inputs, square)


def totals_kernel(scale, sent, _, populations_ref, traces_ref):
    total = jnp.sum(sent[...], axis=0)[:, 0:64]
    populations_ref[...] = total[0:DOM_DEV]
    for n in range(2):
        traces_ref[n] = jnp.sum(total[DOM_DEV + n : DOM_DEV + n + 1]) * scale


def totals(gathered, after, scale):
    return pl.pallas_call(
        functools.partial(totals_kernel, scale),
        in_specs=[pl.BlockSpec(memory_space=pltpu.VMEM), IN_HBM],
        out_specs=[
            pl.BlockSpec(memory_space=pltpu.VMEM),
            pl.BlockSpec(memory_space=pltpu.SMEM),
        ],
        out_shape=[
            jax.ShapeDtypeStruct((DOM_DEV, 64), F32),
            jax.ShapeDtypeStruct((2,), F32),
        ],
        compiler_params=pltpu.CompilerParams(vmem_limit_bytes=16 << 20),
        name="totals",
    )(gathered, after)


def in_hbm(value):
    return pltpu.with_memory_space_constraint(value, pltpu.HBM)


def per_device(density, col_index, counts, domain):
    per_dev, capacity, width = density.shape[:3]
    block_rows = col_index.shape[0]
    radius = (capacity - 1) // 2
    slabs = lax.axis_size("rows")
    devices = slabs * lax.axis_size("layer")
    start = lax.axis_index("rows") * per_dev

    columns = lax.dynamic_slice_in_dim(col_index.T, start, per_dev, 1)
    row_ids = start + jnp.arange(per_dev, dtype=jnp.int32)
    offset = (columns - row_ids[None, :] + radius) % block_rows
    lane = jnp.arange(40, dtype=jnp.int32)
    slots = jnp.arange(capacity, dtype=jnp.int32)
    meta = jnp.sum(
        jnp.where(offset.T[:, :, None] == lane[None, None, :], slots[None, :, None], 0), axis=1
    )

    def device(row, core):
        return (row % slabs) * 2 + core

    ahead = [(device(r, 0), device(r + 1, 0)) for r in range(slabs)]
    ahead += [(device(r, 1), device(r - 1, 1)) for r in range(slabs)]
    across = [(device(r, c), device(r, 1 - c)) for r in range(slabs) for c in range(2)]

    density = in_hbm(density)
    (ss,) = pack(((SYM, 1, 1),), meta, density)
    tiles = ((FULL, 0, 1), (SYM, 0, 0))
    ms, mm, partial = rest(tiles, meta, domain, density, ss, devices)
    ss = lax.ppermute(ss, AXES, ahead)
    ms = lax.ppermute(ms, AXES, ahead)
    mm = lax.ppermute(mm, AXES, ahead)
    gathered = lax.all_to_all(partial, AXES, 0, 0, tiled=True)
    head, others, part, square = local(meta, counts, density, partial)
    corner = lax.ppermute(ss, AXES, across)
    inputs = (head, others, part, ss, ms, corner)
    extra = (jax.ShapeDtypeStruct(head.shape, F32),)
    first, square = closing(middle_kernel, meta, counts, inputs, in_hbm(square), 100, extra, 2, 24)
    inputs = (head, first, mm)
    (square,) = closing(last_kernel, meta, counts, inputs, in_hbm(square), 36, (), 1, 16)
    populations, traces = totals(gathered, in_hbm(square), 1.0 / (block_rows * width))
    return (square, populations, traces)


def solution(mesh):
    placed = (P("rows", None, None, None), P(), P(), P())
    return jax.shard_map(
        per_device,
        mesh=mesh,
        in_specs=placed,
        out_specs=(P(("rows", "layer"), None, None, None), P(("rows", "layer"), None), P()),
        check_vma=False,
    )
```

time: 913 us -> 37.7 us (0.04)
  waiting for transfers between devices: 344 us -> 1.75 us
  matrix products: 262 us -> 0 us
  local copies, waits for them, and re-layouts: 225 us -> 0.01 us
  blocking collectives: 40.2 us -> 0 us
  other arithmetic: 27.2 us -> 0.95 us
  Pallas kernels: 0 us -> 20.3 us
    ppermute x2 -> x4, waiting for transfers between devices: 344 us -> 1.74 us  [the longest x1 1.58 us: per_device(): ss = lax.ppermute(ss, AXES, ahead)]
    dot_general x17 -> x0, matrix products: 262 us -> none  [the longest x8 173 us: row_block(): jnp.einsum('amb,abxy->amxy', select.astype(jnp.bfloat16), partner_rows, p...]
    gather x45 -> x0, local copies, waits for them, and re-layouts: 163 us -> none  [the longest x8 129 us: row_block(): partner_rows = banded[position]]
    unnamed x1 -> x0, blocking collectives: 40.2 us -> none
    unnamed x20 -> x4, local copies, waits for them, and re-layouts: 22.2 us -> 0.01 us
    pallas_call x0 -> x6, Pallas kernels: none -> 20.3 us  [the longest x1 8.51 us: local(): pl.pallas_call(local_kernel, grid_spec=pltpu.PrefetchScalarGridSpec(num_s...]
    concatenate x2 -> x0, other arithmetic: 18.6 us -> none  [the longest x1 18.6 us: padded(): value = jnp.concatenate([before, value, after], axis=dim)]
    while x1 -> x0, local copies, waits for them, and re-layouts: 15.7 us -> none  [per_device(): lax.map(lambda local: row_block(layer_id * half_rows + local, slot_ids),...]
  transfers between devices with their start and end apart: 2 -> 5, of which waited for: 2 -> 2; matrix products, arithmetic and copies ran while one was open for 3% -> 0% of each run, Pallas kernels for 0% -> 48%
where the time goes in v2:
time: 37.7 us; the launch traced here: 37 us
  Pallas kernels  20.3 us (54%)
  starting transfers between devices  13.2 us (35%)
  waiting for transfers between devices  1.75 us (5%)
  other arithmetic  0.95 us (3%)
  between operations  0.75 us (2%)
    pallas_call x1, Pallas kernels, local(): pl.pallas_call(local_kernel, grid_spec=pltpu.PrefetchScalarGridSpec(num_s...  8.51 us
    all_to_all x1, starting transfers between devices, per_device(): gathered = lax.all_to_all(partial, AXES, 0, 0, tiled=True)  4.9 us
    pallas_call x2, Pallas kernels, closing(): pl.pallas_call(kernel, grid_spec=pltpu.PrefetchScalarGridSpec(num_scalar_...  4.73 us
    pallas_call x1, Pallas kernels, rest(): pl.pallas_call(functools.partial(rest_kernel, groups), grid_spec=pltpu.Pr...  4.53 us
    ppermute x1, starting transfers between devices, per_device(): ss = lax.ppermute(ss, AXES, ahead)  3.02 us
    ppermute x1, starting transfers between devices, per_device(): corner = lax.ppermute(ss, AXES, across)  1.97 us
    pallas_call x1, Pallas kernels, pack(): pl.pallas_call(functools.partial(pack_kernel, groups), grid_spec=pltpu.Pr...  1.88 us
    ppermute x1, starting transfers between devices, per_device(): mm = lax.ppermute(mm, AXES, ahead)  1.82 us
  transfers between devices with their start and end apart: 5, of which 2 were waited for; matrix products, arithmetic and copies ran while one was open for 0% of the time, Pallas kernels for 48%

profile of v2, /device:TPU:0, one launch (start us, length us, event | category | flops | bytes accessed | tf_op | source)
XLA Modules:
  0.0 37.0 jit_solution(13051865017701751795)
XLA Ops:
  0.6 0.8 %add_select_fusion = s32[16,33]{0,1:T(8,128)S(1)} fusion(s32[256,33]{0,1:T(8,128)} %param.5, s32[]{:T(128)S(6)} %select_n.15, s32[16]{0:T(128)S(1)} %iota_add_fusion), kind=kLoop, calls=%fused_computation.2 | loop fusion | flops 6864 | bytes 4292 | tf_op jit(solution)/shard_map/jit(remainder)/select_n | solution.py:456
  1.5 0.1 select_reduce_fusion.meta
  1.6 0.0 copy-start.1
  1.6 1.9 %pack.1._ = bf16[10,128,128]{2,1,0:T(8,128)(2,1)S(1)} custom-call(s32[16,40]{1,0:T(8,128)S(1)} %select_reduce_fusion.meta, bf16[16,33,64,64]{3,2,1,0:T(8,128)(2,1)} %density.5), custom_call_target="tpu_custom_call" | custom-call | bytes 1310720 | tf_op jit(solution)/shard_map/pack/pallas_call | solution.py:60
  3.5 0.0 copy-start
  3.5 3.0 %collective-permute-start = (bf16[10,128,128]{2,1,0:T(8,128)(2,1)S(1)}, bf16[10,128,128]{2,1,0:T(8,128)(2,1)S(1)}, u32[]{:S(2)}, u32[]{:S(2)}) collective-permute-start(bf16[10,128,128]{2,1,0:T(8,128)(2,1)S(1)} %pack.1._), channel_id=1, source_target_pairs={{0,2},{2,4},{4,6},{6,8},{8,10},{10,12},{12,14},{14,16},{16,18},{18... | collective-permute-start | bytes 983048 | tf_op jit(solution)/shard_map/ppermute | solution.py:474
  6.5 0.0 copy-done.1
  6.5 4.5 %rest.1 = (bf16[16,128,128]{2,1,0:T(8,128)(2,1)S(1)}, bf16[10,128,128]{2,1,0:T(8,128)(2,1)S(1)}, f32[32,8,128]{2,1,0:T(8,128)}) custom-call(s32[16,40]{1,0:T(8,128)S(1)} %select_reduce_fusion.meta, s32[256]{0:T(256)S(1)} %copy-done.1, bf16[16,33,64,64]{3,2,1,0:T(8,128)(2,1)} %density.5, bf16[10,128,128]{2,1,0:T(8,128)(2,1)S(1)} %pack.1._), custom_call_target="tpu_custom_call" | custom-call | bytes 8388608 | tf_op jit(solution)/shard_map/rest/pallas_call | solution.py:133
  11.1 1.5 %collective-permute-start.1 = (bf16[16,128,128]{2,1,0:T(8,128)(2,1)S(1)}, bf16[16,128,128]{2,1,0:T(8,128)(2,1)S(1)}, u32[]{:S(2)}, u32[]{:S(2)}) collective-permute-start(bf16[16,128,128]{2,1,0:T(8,128)(2,1)S(1)} %get-tuple-element.18), channel_id=1, source_target_pairs={{0,2},{2,4},{4,6},{6,8},{8,10},{10,12},{12,14},{14,16},{16,18},{18... | collective-permute-start | bytes 1572872 | tf_op jit(solution)/shard_map/ppermute | solution.py:475
  12.6 4.9 %all-to-all-start = ((f32[32,8,128]{2,1,0:T(8,128)}), f32[32,8,128]{2,1,0:T(8,128)S(1)}, u32[]{:S(2)}, u32[]{:S(2)}) async-start(f32[32,8,128]{2,1,0:T(8,128)} %get-tuple-element.14._), calls=%async_computation | async-start | bytes 262144 | tf_op jit(solution)/shard_map/all_to_all | solution.py:477
  17.5 1.8 %collective-permute-start.3 = (bf16[10,128,128]{2,1,0:T(8,128)(2,1)S(1)}, bf16[10,128,128]{2,1,0:T(8,128)(2,1)S(1)}, u32[]{:S(2)}, u32[]{:S(2)}) collective-permute-start(bf16[10,128,128]{2,1,0:T(8,128)(2,1)S(1)} %get-tuple-element.21), channel_id=1, source_target_pairs={{0,2},{2,4},{4,6},{6,8},{8,10},{10,12},{12,14},{14,16},{16,18},{18... | collective-permute-start | bytes 983048 | tf_op jit(solution)/shard_map/ppermute | solution.py:476
  19.3 1.6 %collective-permute-done.ss = bf16[10,128,128]{2,1,0:T(8,128)(2,1)S(1)} collective-permute-done((bf16[10,128,128]{2,1,0:T(8,128)(2,1)S(1)}, bf16[10,128,128]{2,1,0:T(8,128)(2,1)S(1)}, u32[]{:S(2)}, u32[]{:S(2)}) %collective-permute-start) | collective-permute-done | bytes 327712 | tf_op jit(solution)/shard_map/ppermute | solution.py:474
  20.9 2.0 %collective-permute-start.2 = (bf16[10,128,128]{2,1,0:T(8,128)(2,1)S(1)}, bf16[10,128,128]{2,1,0:T(8,128)(2,1)S(1)}, u32[]{:S(2)}, u32[]{:S(2)}) collective-permute-start(bf16[10,128,128]{2,1,0:T(8,128)(2,1)S(1)} %collective-permute-done.ss), channel_id=1, source_target_pairs={{0,1},{1,0},{2,3},{3,2},{4,5},{5,4},{6,7},{7,6},{8,9},{9,8},{10,11... | collective-permute-start | bytes 983048 | tf_op jit(solution)/shard_map/ppermute | solution.py:479
  22.9 0.0 copy-done
  22.9 8.5 %local.1 = (bf16[4,512,128]{2,1,0:T(8,128)(2,1)S(1)}, bf16[8,512,128]{2,1,0:T(8,128)(2,1)S(1)}, f32[12,512,128]{2,1,0:T(8,128)S(1)}, bf16[8,33,64,64]{3,2,1,0:T(8,128)(2,1)}) custom-call(s32[16,40]{1,0:T(8,128)S(1)} %select_reduce_fusion.meta, s32[256]{0:T(256)S(1)} %copy-done, bf16[16,33,64,64]{3,2,1,0:T(8,128)(2,1)} %density.5, ...), custom_call_target="tpu_custom_call" | custom-call | flops 4294967296 | bytes 16777216 | tf_op jit(solution)/shard_map/local/pallas_call | solution.py:262
  31.4 0.0 collective-permute-done.1.ms
  31.4 0.0 collective-permute-done.2.corner
  31.4 2.7 %shard_map.67 = (f32[4,512,128]{2,1,0:T(8,128)S(1)}, bf16[8,33,64,64]{3,2,1,0:T(8,128)(2,1)}) custom-call(s32[16,40]{1,0:T(8,128)S(1)} %select_reduce_fusion.meta, s32[256]{0:T(256)S(1)} %copy-done, bf16[4,512,128]{2,1,0:T(8,128)(2,1)S(1)} %get-tuple-element.15.head, ...), custom_call_target="tpu_custom_call", output_to_operand_aliasing={{1}: (8, {})} | custom-call | flops 805306368 | bytes 6291456 | tf_op jit(solution)/shard_map/pallas_call | solution.py:400
  34.1 0.2 collective-permute-done.3.mm
  34.3 2.0 %shard_map.68._ = bf16[8,33,64,64]{3,2,1,0:T(8,128)(2,1)} custom-call(s32[16,40]{1,0:T(8,128)S(1)} %select_reduce_fusion.meta, s32[256]{0:T(256)S(1)} %copy-done, bf16[4,512,128]{2,1,0:T(8,128)(2,1)S(1)} %get-tuple-element.15.head, f32[4,512,128]{2,1,0:T(8,128)S(1)} %get-tuple-element.20.first, ...), custom_call_target="tpu_custom_call", output_to_operand_aliasing={{}: (5, {})} | custom-call | flops 402653184 | bytes 6291456 | tf_op jit(solution)/shard_map/pallas_call | solution.py:400
  36.3 0.0 all-to-all-done.sent
  36.3 0.7 %totals.1 = (f32[2,64]{1,0:T(2,128)}, f32[2]{0:T(128)}) custom-call(f32[32,8,128]{2,1,0:T(8,128)S(1)} %all-to-all-done.sent, bf16[8,33,64,64]{3,2,1,0:T(8,128)(2,1)} %shard_map.68._), custom_call_target="tpu_custom_call" | custom-call | tf_op jit(solution)/shard_map/totals/pallas_call | solution.py:426
  (1 shorter events, 0.0 us)
Async XLA Ops:
  1.6 4.9 %copy-start.1 = (s32[256]{0:T(256)S(1)}, s32[256]{0:T(256)}, u32[]{:S(2)}) copy-start(s32[256]{0:T(256)} %domain.1) | copy-start | bytes 3076
  3.5 19.4 %copy-start = (s32[256]{0:T(256)S(1)}, s32[256]{0:T(256)}, u32[]{:S(2)}) copy-start(s32[256]{0:T(256)} %counts.5) | copy-start | bytes 3076
  3.5 17.4 %collective-permute-start = (bf16[10,128,128]{2,1,0:T(8,128)(2,1)S(1)}, bf16[10,128,128]{2,1,0:T(8,128)(2,1)S(1)}, u32[]{:S(2)}, u32[]{:S(2)}) collective-permute-start(bf16[10,128,128]{2,1,0:T(8,128)(2,1)S(1)} %pack.1._), channel_id=1, source_target_pairs={{0,2},{2,4},{4,6},{6,8},{8,10},{10,12},{12,14},{14,16},{16,18},{18... | collective-permute-start | bytes 983048 | tf_op jit(solution)/shard_map/ppermute | solution.py:474
  11.1 20.3 %collective-permute-start.1 = (bf16[16,128,128]{2,1,0:T(8,128)(2,1)S(1)}, bf16[16,128,128]{2,1,0:T(8,128)(2,1)S(1)}, u32[]{:S(2)}, u32[]{:S(2)}) collective-permute-start(bf16[16,128,128]{2,1,0:T(8,128)(2,1)S(1)} %get-tuple-element.18), channel_id=1, source_target_pairs={{0,2},{2,4},{4,6},{6,8},{8,10},{10,12},{12,14},{14,16},{16,18},{18... | collective-permute-start | bytes 1572872 | tf_op jit(solution)/shard_map/ppermute | solution.py:475
  12.6 23.7 %all-to-all-start = ((f32[32,8,128]{2,1,0:T(8,128)}), f32[32,8,128]{2,1,0:T(8,128)S(1)}, u32[]{:S(2)}, u32[]{:S(2)}) async-start(f32[32,8,128]{2,1,0:T(8,128)} %get-tuple-element.14._), calls=%async_computation | async-start | bytes 262144 | tf_op jit(solution)/shard_map/all_to_all | solution.py:477
  17.5 16.8 %collective-permute-start.3 = (bf16[10,128,128]{2,1,0:T(8,128)(2,1)S(1)}, bf16[10,128,128]{2,1,0:T(8,128)(2,1)S(1)}, u32[]{:S(2)}, u32[]{:S(2)}) collective-permute-start(bf16[10,128,128]{2,1,0:T(8,128)(2,1)S(1)} %get-tuple-element.21), channel_id=1, source_target_pairs={{0,2},{2,4},{4,6},{6,8},{8,10},{10,12},{12,14},{14,16},{16,18},{18... | collective-permute-start | bytes 983048 | tf_op jit(solution)/shard_map/ppermute | solution.py:476
  20.9 10.5 %collective-permute-start.2 = (bf16[10,128,128]{2,1,0:T(8,128)(2,1)S(1)}, bf16[10,128,128]{2,1,0:T(8,128)(2,1)S(1)}, u32[]{:S(2)}, u32[]{:S(2)}) collective-permute-start(bf16[10,128,128]{2,1,0:T(8,128)(2,1)S(1)} %collective-permute-done.ss), channel_id=1, source_target_pairs={{0,1},{1,0},{2,3},{3,2},{4,5},{5,4},{6,7},{7,6},{8,9},{9,8},{10,11... | collective-permute-start | bytes 983048 | tf_op jit(solution)/shard_map/ppermute | solution.py:479

commit v3 on v2

--- a/solution.py
+++ b/solution.py
@@ -10,8 +10,20 @@
 
 DOM_DEV = 2
 AXES = ("rows", "layer")
-SYM = [(u, t) for u in range(4) for t in range(u, 4)]
-FULL = [(u, t) for u in range(4) for t in range(4)]
+
+
+def tile_blocks(u, t):
+    return [(2 * u + r, 2 * t + s) for r in range(2) for s in range(2)]
+
+
+OFF = [(u, t) for u in range(4) for t in range(u + 1, 4)]
+DIAGONAL = [
+    [(0, 0), (0, 1), (2, 2), (2, 3)],
+    [(4, 4), (4, 5), (6, 6), (6, 7)],
+    [(1, 1), (3, 3), (5, 5), (7, 7)],
+]
+SYM = [tile_blocks(u, t) for u, t in OFF] + DIAGONAL
+FULL = [tile_blocks(u, t) for u in range(4) for t in range(4)]
 NT = (((1,), (1,)), ((), ()))
 BF = jnp.bfloat16
 F32 = jnp.float32
@@ -25,13 +37,11 @@
     base = 0
     for g, (tiles, near, far) in enumerate(groups):
         row, col = starts[near], starts[far]
-        for n, (u, t) in enumerate(tiles):
-            for r in range(2):
-                for s in range(2):
-                    k = row + 2 * u + r
-                    slot = meta[k, (col - row) + 2 * t + s - 2 * u - r + 16]
-                    at = base + 4 * n + 2 * r + s
-                    pltpu.make_async_copy(density.at[k, slot], buf.at[at], sems.at[g]).start()
+        for n, blocks in enumerate(tiles):
+            for x, (i, j) in enumerate(blocks):
+                slot = meta[row + i, (col - row) + j - i + 16]
+                source = density.at[row + i, slot]
+                pltpu.make_async_copy(source, buf.at[base + 4 * n + x], sems.at[g]).start()
         base += 4 * len(tiles)
 
 
@@ -291,7 +301,13 @@
 
 
 def corners(tiles_ref):
-    tile = {ut: tiles_ref[n] for n, ut in enumerate(SYM)}
+    tile = {ut: tiles_ref[n] for n, ut in enumerate(OFF)}
+    for u in range(4):
+        top = tiles_ref[6 + u // 2, 64 * (u % 2) : 64 * (u % 2) + 64, :]
+        below = tiles_ref[8, 64 * (u // 2) : 64 * (u // 2) + 64, :]
+        below = below[:, 64 * (u % 2) : 64 * (u % 2) + 64]
+        bottom = jnp.concatenate([top[:, 64:128].T, below], axis=1)
+        tile[u, u] = jnp.concatenate([top, bottom], axis=0)
 
     def square(u):
         top = jnp.concatenate([tile[u, u], tile[u, u + 1]], axis=1)

time: 37.7 us -> 37.6 us (level)
  waiting for transfers between devices: 1.75 us -> 0.2 us
  starting transfers between devices: 13.2 us -> 14.7 us
    ppermute x1, starting transfers between devices: 1.97 us -> 3.36 us  [per_device(): corner = lax.ppermute(ss, AXES, across)]
    ppermute x1, waiting for transfers between devices: 1.58 us -> 0.19 us  [per_device(): ss = lax.ppermute(ss, AXES, ahead)]
  transfers between devices with their start and end apart: 5 -> 5, of which waited for: 2 -> 1; matrix products, arithmetic and copies ran while one was open for 0% -> 0% of each run, Pallas kernels for 48% -> 49%
where the time goes in v3:
time: 37.6 us; the launch traced here: 37.2 us
  Pallas kernels  20.6 us (55%)
  starting transfers between devices  14.7 us (39%)
  other arithmetic  0.95 us (3%)
  between operations  0.75 us (2%)
    pallas_call x1, Pallas kernels, local(): pl.pallas_call(local_kernel, grid_spec=pltpu.PrefetchScalarGridSpec(num_s...  8.52 us
    pallas_call x2, Pallas kernels, closing(): pl.pallas_call(kernel, grid_spec=pltpu.PrefetchScalarGridSpec(num_scalar_...  4.87 us
    all_to_all x1, starting transfers between devices, per_device(): gathered = lax.all_to_all(partial, AXES, 0, 0, tiled=True)  4.83 us
    pallas_call x1, Pallas kernels, rest(): pl.pallas_call(functools.partial(rest_kernel, groups), grid_spec=pltpu.Pr...  4.73 us
    ppermute x1, starting transfers between devices, per_device(): corner = lax.ppermute(ss, AXES, across)  3.36 us
    ppermute x1, starting transfers between devices, per_device(): ss = lax.ppermute(ss, AXES, ahead)  3.02 us
    pallas_call x1, Pallas kernels, pack(): pl.pallas_call(functools.partial(pack_kernel, groups), grid_spec=pltpu.Pr...  1.85 us
    ppermute x1, starting transfers between devices, per_device(): mm = lax.ppermute(mm, AXES, ahead)  1.82 us
  transfers between devices with their start and end apart: 5, of which 1 were waited for; matrix products, arithmetic and copies ran while one was open for 0% of the time, Pallas kernels for 49%

profile of v3, /device:TPU:0, one launch (start us, length us, event | category | flops | bytes accessed | tf_op | source)
XLA Modules:
  0.0 37.2 jit_solution(12772973741503252428)
XLA Ops:
  0.6 0.8 %add_select_fusion = s32[16,33]{0,1:T(8,128)S(1)} fusion(s32[256,33]{0,1:T(8,128)} %param.5, s32[]{:T(128)S(6)} %select_n.15, s32[16]{0:T(128)S(1)} %iota_add_fusion), kind=kLoop, calls=%fused_computation.2 | loop fusion | flops 6864 | bytes 4292 | tf_op jit(solution)/shard_map/jit(remainder)/select_n | solution.py:472
  1.5 0.1 select_reduce_fusion.meta
  1.6 0.0 copy-start.1
  1.6 1.8 %pack.1._ = bf16[9,128,128]{2,1,0:T(8,128)(2,1)S(1)} custom-call(s32[16,40]{1,0:T(8,128)S(1)} %select_reduce_fusion.meta, bf16[16,33,64,64]{3,2,1,0:T(8,128)(2,1)} %density.5), custom_call_target="tpu_custom_call" | custom-call | bytes 1179648 | tf_op jit(solution)/shard_map/pack/pallas_call | solution.py:70
  3.5 0.0 copy-start
  3.5 3.0 %collective-permute-start = (bf16[9,128,128]{2,1,0:T(8,128)(2,1)S(1)}, bf16[9,128,128]{2,1,0:T(8,128)(2,1)S(1)}, u32[]{:S(2)}, u32[]{:S(2)}) collective-permute-start(bf16[9,128,128]{2,1,0:T(8,128)(2,1)S(1)} %pack.1._), channel_id=1, source_target_pairs={{0,2},{2,4},{4,6},{6,8},{8,10},{10,12},{12,14},{14,16},{16,18},{18... | collective-permute-start | bytes 884744 | tf_op jit(solution)/shard_map/ppermute | solution.py:490
  6.5 0.0 copy-done.1
  6.5 4.7 %rest.1 = (bf16[16,128,128]{2,1,0:T(8,128)(2,1)S(1)}, bf16[9,128,128]{2,1,0:T(8,128)(2,1)S(1)}, f32[32,8,128]{2,1,0:T(8,128)}) custom-call(s32[16,40]{1,0:T(8,128)S(1)} %select_reduce_fusion.meta, s32[256]{0:T(256)S(1)} %copy-done.1, bf16[16,33,64,64]{3,2,1,0:T(8,128)(2,1)} %density.5, bf16[9,128,128]{2,1,0:T(8,128)(2,1)S(1)} %pack.1._), custom_call_target="tpu_custom_call" | custom-call | bytes 8388608 | tf_op jit(solution)/shard_map/rest/pallas_call | solution.py:143
  11.3 1.6 %collective-permute-start.1 = (bf16[16,128,128]{2,1,0:T(8,128)(2,1)S(1)}, bf16[16,128,128]{2,1,0:T(8,128)(2,1)S(1)}, u32[]{:S(2)}, u32[]{:S(2)}) collective-permute-start(bf16[16,128,128]{2,1,0:T(8,128)(2,1)S(1)} %get-tuple-element.18), channel_id=1, source_target_pairs={{0,2},{2,4},{4,6},{6,8},{8,10},{10,12},{12,14},{14,16},{16,18},{18... | collective-permute-start | bytes 1572872 | tf_op jit(solution)/shard_map/ppermute | solution.py:491
  12.9 4.8 %all-to-all-start = ((f32[32,8,128]{2,1,0:T(8,128)}), f32[32,8,128]{2,1,0:T(8,128)S(1)}, u32[]{:S(2)}, u32[]{:S(2)}) async-start(f32[32,8,128]{2,1,0:T(8,128)} %get-tuple-element.14._), calls=%async_computation | async-start | bytes 262144 | tf_op jit(solution)/shard_map/all_to_all | solution.py:493
  17.7 1.8 %collective-permute-start.3 = (bf16[9,128,128]{2,1,0:T(8,128)(2,1)S(1)}, bf16[9,128,128]{2,1,0:T(8,128)(2,1)S(1)}, u32[]{:S(2)}, u32[]{:S(2)}) collective-permute-start(bf16[9,128,128]{2,1,0:T(8,128)(2,1)S(1)} %get-tuple-element.21), channel_id=1, source_target_pairs={{0,2},{2,4},{4,6},{6,8},{8,10},{10,12},{12,14},{14,16},{16,18},{18... | collective-permute-start | bytes 884744 | tf_op jit(solution)/shard_map/ppermute | solution.py:492
  19.6 0.2 collective-permute-done.ss
  19.7 3.4 %collective-permute-start.2 = (bf16[9,128,128]{2,1,0:T(8,128)(2,1)S(1)}, bf16[9,128,128]{2,1,0:T(8,128)(2,1)S(1)}, u32[]{:S(2)}, u32[]{:S(2)}) collective-permute-start(bf16[9,128,128]{2,1,0:T(8,128)(2,1)S(1)} %collective-permute-done.ss), channel_id=1, source_target_pairs={{0,1},{1,0},{2,3},{3,2},{4,5},{5,4},{6,7},{7,6},{8,9},{9,8},{10,11... | collective-permute-start | bytes 884744 | tf_op jit(solution)/shard_map/ppermute | solution.py:495
  23.1 0.0 copy-done
  23.1 8.5 %local.1 = (bf16[4,512,128]{2,1,0:T(8,128)(2,1)S(1)}, bf16[8,512,128]{2,1,0:T(8,128)(2,1)S(1)}, f32[12,512,128]{2,1,0:T(8,128)S(1)}, bf16[8,33,64,64]{3,2,1,0:T(8,128)(2,1)}) custom-call(s32[16,40]{1,0:T(8,128)S(1)} %select_reduce_fusion.meta, s32[256]{0:T(256)S(1)} %copy-done, bf16[16,33,64,64]{3,2,1,0:T(8,128)(2,1)} %density.5, ...), custom_call_target="tpu_custom_call" | custom-call | flops 4294967296 | bytes 16777216 | tf_op jit(solution)/shard_map/local/pallas_call | solution.py:272
  31.6 0.0 collective-permute-done.1.ms
  31.6 0.0 collective-permute-done.2.corner
  31.7 2.9 %shard_map.67 = (f32[4,512,128]{2,1,0:T(8,128)S(1)}, bf16[8,33,64,64]{3,2,1,0:T(8,128)(2,1)}) custom-call(s32[16,40]{1,0:T(8,128)S(1)} %select_reduce_fusion.meta, s32[256]{0:T(256)S(1)} %copy-done, bf16[4,512,128]{2,1,0:T(8,128)(2,1)S(1)} %get-tuple-element.15.head, ...), custom_call_target="tpu_custom_call", output_to_operand_aliasing={{1}: (8, {})} | custom-call | flops 805306368 | bytes 6291456 | tf_op jit(solution)/shard_map/pallas_call | solution.py:416
  34.5 0.0 collective-permute-done.3.mm
  34.5 2.0 %shard_map.68._ = bf16[8,33,64,64]{3,2,1,0:T(8,128)(2,1)} custom-call(s32[16,40]{1,0:T(8,128)S(1)} %select_reduce_fusion.meta, s32[256]{0:T(256)S(1)} %copy-done, bf16[4,512,128]{2,1,0:T(8,128)(2,1)S(1)} %get-tuple-element.15.head, f32[4,512,128]{2,1,0:T(8,128)S(1)} %get-tuple-element.20.first, ...), custom_call_target="tpu_custom_call", output_to_operand_aliasing={{}: (5, {})} | custom-call | flops 402653184 | bytes 6291456 | tf_op jit(solution)/shard_map/pallas_call | solution.py:416
  36.6 0.0 all-to-all-done.sent
  36.6 0.7 %totals.1 = (f32[2,64]{1,0:T(2,128)}, f32[2]{0:T(128)}) custom-call(f32[32,8,128]{2,1,0:T(8,128)S(1)} %all-to-all-done.sent, bf16[8,33,64,64]{3,2,1,0:T(8,128)(2,1)} %shard_map.68._), custom_call_target="tpu_custom_call" | custom-call | tf_op jit(solution)/shard_map/totals/pallas_call | solution.py:442
  (1 shorter events, 0.0 us)
Async XLA Ops:
  1.6 4.9 %copy-start.1 = (s32[256]{0:T(256)S(1)}, s32[256]{0:T(256)}, u32[]{:S(2)}) copy-start(s32[256]{0:T(256)} %domain.1) | copy-start | bytes 3076
  3.5 19.6 %copy-start = (s32[256]{0:T(256)S(1)}, s32[256]{0:T(256)}, u32[]{:S(2)}) copy-start(s32[256]{0:T(256)} %counts.5) | copy-start | bytes 3076
  3.5 16.2 %collective-permute-start = (bf16[9,128,128]{2,1,0:T(8,128)(2,1)S(1)}, bf16[9,128,128]{2,1,0:T(8,128)(2,1)S(1)}, u32[]{:S(2)}, u32[]{:S(2)}) collective-permute-start(bf16[9,128,128]{2,1,0:T(8,128)(2,1)S(1)} %pack.1._), channel_id=1, source_target_pairs={{0,2},{2,4},{4,6},{6,8},{8,10},{10,12},{12,14},{14,16},{16,18},{18... | collective-permute-start | bytes 884744 | tf_op jit(solution)/shard_map/ppermute | solution.py:490
  11.3 20.4 %collective-permute-start.1 = (bf16[16,128,128]{2,1,0:T(8,128)(2,1)S(1)}, bf16[16,128,128]{2,1,0:T(8,128)(2,1)S(1)}, u32[]{:S(2)}, u32[]{:S(2)}) collective-permute-start(bf16[16,128,128]{2,1,0:T(8,128)(2,1)S(1)} %get-tuple-element.18), channel_id=1, source_target_pairs={{0,2},{2,4},{4,6},{6,8},{8,10},{10,12},{12,14},{14,16},{16,18},{18... | collective-permute-start | bytes 1572872 | tf_op jit(solution)/shard_map/ppermute | solution.py:491
  12.9 23.7 %all-to-all-start = ((f32[32,8,128]{2,1,0:T(8,128)}), f32[32,8,128]{2,1,0:T(8,128)S(1)}, u32[]{:S(2)}, u32[]{:S(2)}) async-start(f32[32,8,128]{2,1,0:T(8,128)} %get-tuple-element.14._), calls=%async_computation | async-start | bytes 262144 | tf_op jit(solution)/shard_map/all_to_all | solution.py:493
  17.7 16.8 %collective-permute-start.3 = (bf16[9,128,128]{2,1,0:T(8,128)(2,1)S(1)}, bf16[9,128,128]{2,1,0:T(8,128)(2,1)S(1)}, u32[]{:S(2)}, u32[]{:S(2)}) collective-permute-start(bf16[9,128,128]{2,1,0:T(8,128)(2,1)S(1)} %get-tuple-element.21), channel_id=1, source_target_pairs={{0,2},{2,4},{4,6},{6,8},{8,10},{10,12},{12,14},{14,16},{16,18},{18... | collective-permute-start | bytes 884744 | tf_op jit(solution)/shard_map/ppermute | solution.py:492
  19.7 11.9 %collective-permute-start.2 = (bf16[9,128,128]{2,1,0:T(8,128)(2,1)S(1)}, bf16[9,128,128]{2,1,0:T(8,128)(2,1)S(1)}, u32[]{:S(2)}, u32[]{:S(2)}) collective-permute-start(bf16[9,128,128]{2,1,0:T(8,128)(2,1)S(1)} %collective-permute-done.ss), channel_id=1, source_target_pairs={{0,1},{1,0},{2,3},{3,2},{4,5},{5,4},{6,7},{7,6},{8,9},{9,8},{10,11... | collective-permute-start | bytes 884744 | tf_op jit(solution)/shard_map/ppermute | solution.py:495

commit v4 on v3

--- a/solution.py
+++ b/solution.py
@@ -148,8 +148,8 @@
             in_specs=[IN_HBM, IN_HBM],
             out_specs=[pl.BlockSpec(shape, lambda i, m, d: (0, 0, 0)) for shape in shapes],
             scratch_shapes=[
-                pltpu.VMEM((4 * sum(sizes), 64, 64), BF),
-                pltpu.SemaphoreType.DMA((len(sizes),)),
+                pltpu.VMEM((max(4 * sum(sizes), 1), 64, 64), BF),
+                pltpu.SemaphoreType.DMA((max(len(sizes), 1),)),
                 pltpu.VMEM((8, capacity, 64, 64), BF),
                 pltpu.SemaphoreType.DMA((4,)),
                 pltpu.VMEM((8, 128), F32),
@@ -486,7 +486,8 @@
     density = in_hbm(density)
     (ss,) = pack(((SYM, 1, 1),), meta, density)
     tiles = ((FULL, 0, 1), (SYM, 0, 0))
-    ms, mm, partial = rest(tiles, meta, domain, density, ss, devices)
+    ms, mm = pack(tiles, meta, density)
+    (partial,) = rest((), meta, domain, density, mm, devices)
     ss = lax.ppermute(ss, AXES, ahead)
     ms = lax.ppermute(ms, AXES, ahead)
     mm = lax.ppermute(mm, AXES, ahead)

time: 37.6 us -> 38.4 us (1.021)
  the two profiles are of different devices: /device:TPU:0 before, /device:TPU:27 now
where the time goes in v4:
time: 38.4 us; the launch traced here: 38 us
  Pallas kernels  21.9 us (57%)
  starting transfers between devices  14.4 us (38%)
  other arithmetic  0.95 us (2%)
  between operations  0.76 us (2%)
    pallas_call x1, Pallas kernels, local(): pl.pallas_call(local_kernel, grid_spec=pltpu.PrefetchScalarGridSpec(num_s...  8.53 us
    all_to_all x1, starting transfers between devices, per_device(): gathered = lax.all_to_all(partial, AXES, 0, 0, tiled=True)  7.05 us
    pallas_call x2, Pallas kernels, closing(): pl.pallas_call(kernel, grid_spec=pltpu.PrefetchScalarGridSpec(num_scalar_...  4.88 us
    ppermute x1, starting transfers between devices, per_device(): corner = lax.ppermute(ss, AXES, across)  4.66 us
    pallas_call x2, Pallas kernels, pack(): pl.pallas_call(functools.partial(pack_kernel, groups), grid_spec=pltpu.Pr...  4.09 us
    pallas_call x1, Pallas kernels, rest(): pl.pallas_call(functools.partial(rest_kernel, groups), grid_spec=pltpu.Pr...  3.74 us
    ppermute x1, starting transfers between devices, per_device(): ms = lax.ppermute(ms, AXES, ahead)  2.1 us
    select_n x1, other arithmetic, per_device(): offset = (columns - row_ids[None, :] + radius) % block_rows  0.82 us
  transfers between devices with their start and end apart: 5, of which 0 were waited for; matrix products, arithmetic and copies ran while one was open for 0% of the time, Pallas kernels for 51%

profile of v4, /device:TPU:27, one launch (start us, length us, event | category | flops | bytes accessed | tf_op | source)
XLA Modules:
  0.0 38.0 jit_solution(4286629203971941638)
XLA Ops:
  0.6 0.8 %add_select_fusion = s32[16,33]{0,1:T(8,128)S(1)} fusion(s32[256,33]{0,1:T(8,128)} %param.5, s32[]{:T(128)S(6)} %select_n.15, s32[16]{0:T(128)S(1)} %iota_add_fusion), kind=kLoop, calls=%fused_computation.2 | loop fusion | flops 6864 | bytes 4292 | tf_op jit(solution)/shard_map/jit(remainder)/select_n | solution.py:472
  1.5 0.1 select_reduce_fusion.meta
  1.6 1.8 %pack.3 = bf16[9,128,128]{2,1,0:T(8,128)(2,1)S(1)} custom-call(s32[16,40]{1,0:T(8,128)S(1)} %select_reduce_fusion.meta, bf16[16,33,64,64]{3,2,1,0:T(8,128)(2,1)} %density.7), custom_call_target="tpu_custom_call" | custom-call | bytes 1179648 | tf_op jit(solution)/shard_map/pack/pallas_call | solution.py:70
  3.5 0.0 copy-start.1
  3.5 0.3 collective-permute-start
  3.8 2.2 %pack.2 = (bf16[16,128,128]{2,1,0:T(8,128)(2,1)S(1)}, bf16[9,128,128]{2,1,0:T(8,128)(2,1)S(1)}) custom-call(s32[16,40]{1,0:T(8,128)S(1)} %select_reduce_fusion.meta, bf16[16,33,64,64]{3,2,1,0:T(8,128)(2,1)} %density.7), custom_call_target="tpu_custom_call" | custom-call | bytes 3276800 | tf_op jit(solution)/shard_map/pack/pallas_call | solution.py:70
  6.0 2.1 %collective-permute-start.1 = (bf16[16,128,128]{2,1,0:T(8,128)(2,1)S(1)}, bf16[16,128,128]{2,1,0:T(8,128)(2,1)S(1)}, u32[]{:S(2)}, u32[]{:S(2)}) collective-permute-start(bf16[16,128,128]{2,1,0:T(8,128)(2,1)S(1)} %get-tuple-element.17), channel_id=1, source_target_pairs={{0,2},{2,4},{4,6},{6,8},{8,10},{10,12},{12,14},{14,16},{16,18},{18... | collective-permute-start | bytes 1572872 | tf_op jit(solution)/shard_map/ppermute | solution.py:492
  8.1 0.0 copy-start
  8.1 0.3 collective-permute-start.3
  8.4 0.0 copy-done.1
  8.4 3.7 %rest.1._ = f32[32,8,128]{2,1,0:T(8,128)} custom-call(s32[16,40]{1,0:T(8,128)S(1)} %select_reduce_fusion.meta, s32[256]{0:T(256)S(1)} %copy-done.1, bf16[16,33,64,64]{3,2,1,0:T(8,128)(2,1)} %density.7, bf16[9,128,128]{2,1,0:T(8,128)(2,1)S(1)} %get-tuple-element.13._), custom_call_target="tpu_custom_call" | custom-call | bytes 8388608 | tf_op jit(solution)/shard_map/rest/pallas_call | solution.py:143
  12.1 7.0 %all-to-all-start = ((f32[32,8,128]{2,1,0:T(8,128)}), f32[32,8,128]{2,1,0:T(8,128)S(1)}, u32[]{:S(2)}, u32[]{:S(2)}) async-start(f32[32,8,128]{2,1,0:T(8,128)} %rest.1._), calls=%async_computation | async-start | bytes 262144 | tf_op jit(solution)/shard_map/all_to_all | solution.py:494
  19.2 0.0 collective-permute-done.ss
  19.2 4.7 %collective-permute-start.2 = (bf16[9,128,128]{2,1,0:T(8,128)(2,1)S(1)}, bf16[9,128,128]{2,1,0:T(8,128)(2,1)S(1)}, u32[]{:S(2)}, u32[]{:S(2)}) collective-permute-start(bf16[9,128,128]{2,1,0:T(8,128)(2,1)S(1)} %collective-permute-done.ss), channel_id=1, source_target_pairs={{0,1},{1,0},{2,3},{3,2},{4,5},{5,4},{6,7},{7,6},{8,9},{9,8},{10,11... | collective-permute-start | bytes 884744 | tf_op jit(solution)/shard_map/ppermute | solution.py:496
  23.9 0.0 copy-done
  23.9 8.5 %local.1 = (bf16[4,512,128]{2,1,0:T(8,128)(2,1)S(1)}, bf16[8,512,128]{2,1,0:T(8,128)(2,1)S(1)}, f32[12,512,128]{2,1,0:T(8,128)S(1)}, bf16[8,33,64,64]{3,2,1,0:T(8,128)(2,1)}) custom-call(s32[16,40]{1,0:T(8,128)S(1)} %select_reduce_fusion.meta, s32[256]{0:T(256)S(1)} %copy-done, bf16[16,33,64,64]{3,2,1,0:T(8,128)(2,1)} %density.7, f32[32,8,128]{2,1,0:T(8,128)} %rest.1._), custom_call_target="tpu_custom_call" | custom-call | flops 4294967296 | bytes 16777216 | tf_op jit(solution)/shard_map/local/pallas_call | solution.py:272
  32.4 0.0 collective-permute-done.1.ms
  32.4 0.0 collective-permute-done.2.corner
  32.4 2.9 %shard_map.67 = (f32[4,512,128]{2,1,0:T(8,128)S(1)}, bf16[8,33,64,64]{3,2,1,0:T(8,128)(2,1)}) custom-call(s32[16,40]{1,0:T(8,128)S(1)} %select_reduce_fusion.meta, s32[256]{0:T(256)S(1)} %copy-done, bf16[4,512,128]{2,1,0:T(8,128)(2,1)S(1)} %get-tuple-element.14.head, ...), custom_call_target="tpu_custom_call", output_to_operand_aliasing={{1}: (8, {})} | custom-call | flops 805306368 | bytes 6291456 | tf_op jit(solution)/shard_map/pallas_call | solution.py:416
  35.3 0.0 collective-permute-done.3.mm
  35.3 2.0 %shard_map.68._ = bf16[8,33,64,64]{3,2,1,0:T(8,128)(2,1)} custom-call(s32[16,40]{1,0:T(8,128)S(1)} %select_reduce_fusion.meta, s32[256]{0:T(256)S(1)} %copy-done, bf16[4,512,128]{2,1,0:T(8,128)(2,1)S(1)} %get-tuple-element.14.head, f32[4,512,128]{2,1,0:T(8,128)S(1)} %get-tuple-element.19.first, ...), custom_call_target="tpu_custom_call", output_to_operand_aliasing={{}: (5, {})} | custom-call | flops 402653184 | bytes 6291456 | tf_op jit(solution)/shard_map/pallas_call | solution.py:416
  37.3 0.0 all-to-all-done.sent
  37.4 0.7 %totals.1 = (f32[2,64]{1,0:T(2,128)}, f32[2]{0:T(128)}) custom-call(f32[32,8,128]{2,1,0:T(8,128)S(1)} %all-to-all-done.sent, bf16[8,33,64,64]{3,2,1,0:T(8,128)(2,1)} %shard_map.68._), custom_call_target="tpu_custom_call" | custom-call | tf_op jit(solution)/shard_map/totals/pallas_call | solution.py:442
  (1 shorter events, 0.0 us)
Async XLA Ops:
  3.5 4.9 %copy-start.1 = (s32[256]{0:T(256)S(1)}, s32[256]{0:T(256)}, u32[]{:S(2)}) copy-start(s32[256]{0:T(256)} %domain.1) | copy-start | bytes 3076
  3.5 15.7 %collective-permute-start = (bf16[9,128,128]{2,1,0:T(8,128)(2,1)S(1)}, bf16[9,128,128]{2,1,0:T(8,128)(2,1)S(1)}, u32[]{:S(2)}, u32[]{:S(2)}) collective-permute-start(bf16[9,128,128]{2,1,0:T(8,128)(2,1)S(1)} %pack.3), channel_id=1, source_target_pairs={{0,2},{2,4},{4,6},{6,8},{8,10},{10,12},{12,14},{14,16},{16,18},{18... | collective-permute-start | bytes 884744 | tf_op jit(solution)/shard_map/ppermute | solution.py:491
  6.0 26.4 %collective-permute-start.1 = (bf16[16,128,128]{2,1,0:T(8,128)(2,1)S(1)}, bf16[16,128,128]{2,1,0:T(8,128)(2,1)S(1)}, u32[]{:S(2)}, u32[]{:S(2)}) collective-permute-start(bf16[16,128,128]{2,1,0:T(8,128)(2,1)S(1)} %get-tuple-element.17), channel_id=1, source_target_pairs={{0,2},{2,4},{4,6},{6,8},{8,10},{10,12},{12,14},{14,16},{16,18},{18... | collective-permute-start | bytes 1572872 | tf_op jit(solution)/shard_map/ppermute | solution.py:492
  8.1 15.7 %copy-start = (s32[256]{0:T(256)S(1)}, s32[256]{0:T(256)}, u32[]{:S(2)}) copy-start(s32[256]{0:T(256)} %counts.5) | copy-start | bytes 3076
  8.1 27.2 %collective-permute-start.3 = (bf16[9,128,128]{2,1,0:T(8,128)(2,1)S(1)}, bf16[9,128,128]{2,1,0:T(8,128)(2,1)S(1)}, u32[]{:S(2)}, u32[]{:S(2)}) collective-permute-start(bf16[9,128,128]{2,1,0:T(8,128)(2,1)S(1)} %get-tuple-element.13._), channel_id=1, source_target_pairs={{0,2},{2,4},{4,6},{6,8},{8,10},{10,12},{12,14},{14,16},{16,18},{18... | collective-permute-start | bytes 884744 | tf_op jit(solution)/shard_map/ppermute | solution.py:493
  12.1 25.2 %all-to-all-start = ((f32[32,8,128]{2,1,0:T(8,128)}), f32[32,8,128]{2,1,0:T(8,128)S(1)}, u32[]{:S(2)}, u32[]{:S(2)}) async-start(f32[32,8,128]{2,1,0:T(8,128)} %rest.1._), calls=%async_computation | async-start | bytes 262144 | tf_op jit(solution)/shard_map/all_to_all | solution.py:494
  19.2 13.2 %collective-permute-start.2 = (bf16[9,128,128]{2,1,0:T(8,128)(2,1)S(1)}, bf16[9,128,128]{2,1,0:T(8,128)(2,1)S(1)}, u32[]{:S(2)}, u32[]{:S(2)}) collective-permute-start(bf16[9,128,128]{2,1,0:T(8,128)(2,1)S(1)} %collective-permute-done.ss), channel_id=1, source_target_pairs={{0,1},{1,0},{2,3},{3,2},{4,5},{5,4},{6,7},{7,6},{8,9},{9,8},{10,11... | collective-permute-start | bytes 884744 | tf_op jit(solution)/shard_map/ppermute | solution.py:496
